TPU v7x, 512 devices: a whole 4x4x16 slice. The times are simulated.
512 devices in a mesh: dp: 16 (over y, x), tensor: 32 (over z, core).
Axes of the slice: x: 4, y: 4, z: 16, core: 2. Of those that a mesh axis runs over, the one named last changes fastest.
Arguments:
- inputs: bfloat16 [2048, 4096], P('dp', 'tensor'), may hold values from -6 to 6
- cotangent: bfloat16 [2048, 4096], P('dp', 'tensor'), may hold values from -6 to 6
- gate_w: bfloat16 [32, 24, 128, 128], P('tensor'), may hold values from -0.25 to 0.25
- up_w: bfloat16 [32, 24, 128, 128], P('tensor'), may hold values from -0.25 to 0.25
- down_w: bfloat16 [32, 24, 128, 128], P('tensor'), may hold values from -0.25 to 0.25
- gate_list: int32 [32, 24], P('tensor'), may hold values from -1 to 127, as said below
- up_list: int32 [32, 24], P('tensor'), may hold values from -1 to 127, as said below
- down_list: int32 [32, 24], P('tensor'), may hold values from -1 to 127, as said below
Outputs:
- grad_x: bfloat16 [2048, 4096], P('dp', 'tensor')
- grad_gate_w: bfloat16 [32, 24, 128, 128], P('tensor', None, 'dp')
- grad_up_w: bfloat16 [32, 24, 128, 128], P('tensor', None, 'dp')
- grad_down_w: bfloat16 [32, 24, 128, 128], P('tensor', None, 'dp')
Inputs may be any that keep to these rules, and one draw needn't show every extreme that they name: `gate_list`: row j of the list names blocks of hidden blocks j * 4 to j * 4 + 3 only; no entry appears twice in a row; live entries come first and -1 fills the rest; a row holds at most 24 live entries and some row holds exactly 24. `up_list`: as for gate_list, drawn independently. `down_list`: as for gate_list, drawn independently.
All inputs are finite; a program needn't handle non-finite values.
Results may differ from a plain program's by a relative error of at most 0.014.
Values may be sent and summed in bfloat16 or wider, within the bound.
No kernel may reach another device: no remote copies, remote signals or barrier semaphores. Data moves between devices by JAX's collectives and lax.ppermute only.
A program may use at most 64 MiB of HBM per device.

v0:
```python
import math

import jax
import jax.numpy as jnp
from jax import lax
from jax.sharding import PartitionSpec as P

D = 4096
FF = 16384
BLOCK = 128


def decode(entries, row_count):
    living = entries >= 0
    clamped = jnp.maximum(entries, 0)
    return (living, clamped // row_count, clamped % row_count)


def one_hot(block_index, width_count, living):
    return ((block_index[:, None] == jnp.arange(width_count)[None, :]) & living[:, None]).astype(
        jnp.float32
    )


def select_sum(values, table):
    return jnp.sum(values[:, :, None, :] * table[None, :, :, None], axis=1)


def project_rows(blocks_in, weights, rows_hot):
    products = jnp.einsum("tkc,kch->tkh", blocks_in, weights, preferred_element_type=jnp.float32)
    return select_sum(products, rows_hot)


def weight_term(products, grad_scale, living):
    rounded = (products * grad_scale).astype(jnp.bfloat16)
    rounded = lax.optimization_barrier(rounded)
    return (rounded.astype(jnp.float32) * living[:, None, None].astype(jnp.float32))[None]


def add_sources(received):
    return jnp.sum(received.astype(jnp.float32), axis=1)


def on_device(inputs, cotangent, gate_w, up_w, down_w, gate_list, up_list, down_list):
    tensor_size = lax.axis_size("tensor")
    hidden_rows = FF // (BLOCK * tensor_size)
    feat_blocks = D // BLOCK
    tokens_here = inputs.shape[0]
    grad_scale = 1.0 / math.sqrt(tokens_here * lax.axis_size("dp"))
    gate_live, gate_feat, gate_row = decode(gate_list[0], hidden_rows)
    up_live, up_feat, up_row = decode(up_list[0], hidden_rows)
    down_live, down_feat, down_row = decode(down_list[0], hidden_rows)
    whole_in, whole_cot = (
        lax.all_gather(inputs, "tensor", axis=1, tiled=True),
        lax.all_gather(cotangent, "tensor", axis=1, tiled=True),
    )
    input_blocks = whole_in.reshape(tokens_here, feat_blocks, BLOCK)
    gate_in = jnp.take(input_blocks, gate_feat, axis=1)
    up_in = jnp.take(input_blocks, up_feat, axis=1)
    gate_val = project_rows(gate_in, gate_w[0], one_hot(gate_row, hidden_rows, gate_live))
    up_val = project_rows(up_in, up_w[0], one_hot(up_row, hidden_rows, up_live))
    sigmoid_gate = jax.nn.sigmoid(gate_val)
    active = gate_val * sigmoid_gate
    hidden = (active * up_val).astype(jnp.bfloat16)
    cot_blocks = whole_cot.reshape(tokens_here, feat_blocks, BLOCK)
    down_cot = jnp.take(cot_blocks, down_feat, axis=1)
    hidden_down = jnp.take(hidden, down_row, axis=1)
    down_part = jnp.einsum("tkc,khc->tkh", down_cot, down_w[0], preferred_element_type=jnp.float32)
    grad_hidden = select_sum(down_part, one_hot(down_row, hidden_rows, down_live))
    down_term = weight_term(
        jnp.einsum("tkh,tkc->khc", hidden_down, down_cot, preferred_element_type=jnp.float32),
        grad_scale,
        down_live,
    )
    grad_gate = (
        grad_hidden * up_val * sigmoid_gate * (1.0 + gate_val * (1.0 - sigmoid_gate))
    ).astype(jnp.bfloat16)
    grad_up = (grad_hidden * active).astype(jnp.bfloat16)
    gate_back = jnp.take(grad_gate, gate_row, axis=1)
    up_back = jnp.take(grad_up, up_row, axis=1)
    gate_term = weight_term(
        jnp.einsum("tkc,tkh->kch", gate_in, gate_back, preferred_element_type=jnp.float32),
        grad_scale,
        gate_live,
    )
    up_term = weight_term(
        jnp.einsum("tkc,tkh->kch", up_in, up_back, preferred_element_type=jnp.float32),
        grad_scale,
        up_live,
    )
    back_gate = jnp.einsum("tkh,kch->tkc", gate_back, gate_w[0], preferred_element_type=jnp.float32)
    back_up = jnp.einsum("tkh,kch->tkc", up_back, up_w[0], preferred_element_type=jnp.float32)
    partial_sum = select_sum(back_gate, one_hot(gate_feat, feat_blocks, gate_live))
    partial_sum = partial_sum + select_sum(back_up, one_hot(up_feat, feat_blocks, up_live))
    pieces = partial_sum.astype(jnp.bfloat16)
    summed = add_sources(lax.all_to_all(pieces, "tensor", split_axis=1, concat_axis=1, tiled=True))
    grad_x = summed.astype(jnp.bfloat16)
    gate_sum, up_sum, down_sum = (
        lax.psum_scatter(
            gate_term.astype(jnp.bfloat16), "dp", scatter_dimension=2, tiled=True
        ).astype(jnp.float32),
        lax.psum_scatter(
            up_term.astype(jnp.bfloat16), "dp", scatter_dimension=2, tiled=True
        ).astype(jnp.float32),
        lax.psum_scatter(
            down_term.astype(jnp.bfloat16), "dp", scatter_dimension=2, tiled=True
        ).astype(jnp.float32),
    )
    return (
        grad_x,
        gate_sum.astype(jnp.bfloat16),
        up_sum.astype(jnp.bfloat16),
        down_sum.astype(jnp.bfloat16),
    )


def solution(mesh):
    return jax.shard_map(
        on_device,
        mesh=mesh,
        in_specs=(
            P("dp", "tensor"),
            P("dp", "tensor"),
            P("tensor", None, None, None),
            P("tensor", None, None, None),
            P("tensor", None, None, None),
            P("tensor", None),
            P("tensor", None),
            P("tensor", None),
        ),
        out_specs=(
            P("dp", "tensor"),
            P("tensor", None, "dp", None),
            P("tensor", None, "dp", None),
            P("tensor", None, "dp", None),
        ),
        check_vma=False,
    )
```

profile of v0, /device:TPU:32, one launch (start us, length us, event | category | flops | bytes accessed | tf_op | source)
XLA Modules:
  0.0 357.0 jit_solution(7031194713557921426)
XLA Ops:
  7.2 1.5 copy.56
  8.8 1.5 copy.53
  11.0 1.2 fusion.45
  12.3 1.2 compare_and_fusion.2
  13.5 1.2 fusion.46
  14.8 1.2 compare_and_fusion.5
  16.6 1.2 fusion.44
  18.6 66.7 %all-gather.5.cloned.1.call-done = bf16[128,4096]{0,1:T(8,128)(2,1)} async-done(((bf16[128,128]{0,1:T(8,128)(2,1)}), bf16[128,4096]{0,1:T(8,128)(2,1)}) %all-gather.5.cloned.1.call-update) | async-done | bytes 1048592 | tf_op jit(solution)/shard_map/all_gather | solution.py:54
  85.2 1.6 copy.57
  89.8 1.6 gather_fusion.2
  91.4 1.8 convolution_bitcast_fusion.2
  93.2 2.1 copy.62
  95.2 60.6 %all-gather.3.cloned.1.call-done = bf16[128,4096]{0,1:T(8,128)(2,1)} async-done(((bf16[128,128]{0,1:T(8,128)(2,1)}), bf16[128,4096]{0,1:T(8,128)(2,1)}) %all-gather.3.cloned.1.call-update) | async-done | bytes 1048592 | tf_op jit(solution)/shard_map/all_gather | solution.py:55
  155.8 1.8 copy.54
  157.6 1.6 gather_fusion
  159.2 2.1 convolution_bitcast_fusion.4
  162.2 1.8 multiply_reduce_fusion.4
  164.0 3.5 multiply_reduce_fusion.2
  171.0 2.1 convolution_bitcast_fusion.1
  174.1 13.1 %multiply_reduce_fusion = f32[128,32,128]{2,1,0:T(8,128)S(1)} fusion(f32[24,32]{1,0:T(8,128)S(1)} %fusion.26, f32[128,24,128]{2,1,0:T(8,128)S(1)} %copy.68), kind=kLoop, calls=%fused_computation.6 | loop fusion | flops 24641536 | bytes 3673088 | tf_op jit(solution)/shard_map/reduce_sum | solution.py:26
  187.2 13.3 %multiply_reduce_fusion.1 = f32[128,32,128]{2,1,0:T(8,128)S(1)} fusion(f32[24,32]{1,0:T(8,128)S(1)} %copy-done.11, f32[128,24,128]{2,1,0:T(8,128)S(1)} %copy.65), kind=kLoop, calls=%fused_computation.7 | loop fusion | flops 24641536 | bytes 3673088 | tf_op jit(solution)/shard_map/reduce_sum | solution.py:26
  201.1 1.4 copy.69
  202.5 9.0 %all-to-all-start = ((bf16[128,32,128]{2,0,1:T(8,128)(2,1)}), bf16[128,32,128]{2,0,1:T(8,128)(2,1)S(1)}, u32[]{:S(2)}, u32[]{:S(2)}) async-start(bf16[128,32,128]{2,0,1:T(8,128)(2,1)} %copy.69), calls=%async_computation | async-start | bytes 2097152 | tf_op jit(solution)/shard_map/all_to_all | solution.py:96
  211.6 2.6 multiply_convert_fusion.3
  214.3 1.4 multiply_convert_fusion.5
  219.1 1.1 fusion
  220.2 1.1 fusion.2
  221.4 1.3 dynamic-slice
  223.3 122.1 %all-reduce.6.cloned.1.call-done = (bf16[1,24,128,128]{3,2,1,0:T(8,128)(2,1)}, bf16[1,24,128,128]{3,2,1,0:T(8,128)(2,1)}, bf16[1,24,128,128]{3,2,1,0:T(8,128)(2,1)}) async-done(((bf16[1,24,128,128]{3,2,1,0:T(8,128)(2,1)}, bf16[1,24,128,128]{3,2,1,0:T(8,128)(2,1)}, bf16[1,24,128,128]{3,2,1,0:T(8,128)(2,1)}), (bf16[1,24,128,128]{3,2,1,0:T(8,128)(2,1)}, bf16[1,24,128,128]{3,2,1,0:T(8,128)(2,1)}, ...) | async-done | bytes 2359312
  345.4 1.4 constant_dynamic-slice_fusion
  346.9 1.4 constant_dynamic-slice_fusion.1
  348.3 1.4 constant_dynamic-slice_fusion.2
  (91 shorter events, 15.1 us)
Async XLA Ops:
  7.2 81.3 %copy-start = (bf16[1,24,128,128]{3,2,1,0:T(8,128)(2,1)S(1)}, bf16[1,24,128,128]{3,2,1,0:T(8,128)(2,1)}, u32[]{:S(2)}) copy-start(bf16[1,24,128,128]{3,2,1,0:T(8,128)(2,1)} %param.15) | copy-start | bytes 2359300
  7.2 78.1 %all-gather.5.cloned.1.call-start = ((), (), s32[]{:S(2)}) async-start(), calls=%async_computation.2 | async-start | bytes 1081344 | tf_op jit(solution)/shard_map/all_gather | solution.py:54
  8.8 147.0 %all-gather.3.cloned.1.call-start = ((), (), s32[]{:S(2)}) async-start(), calls=%async_computation.1 | async-start | bytes 1081344 | tf_op jit(solution)/shard_map/all_gather | solution.py:55
  11.0 76.6 %copy-start.12 = (pred[24]{0:T(512)(128)(4,1)}, pred[24]{0:T(512)(128)(4,1)S(1)}, u32[]{:S(2)}) copy-start(pred[24]{0:T(512)(128)(4,1)S(1)} %get-tuple-element.17) | copy-start | bytes 76
  11.0 157.4 %copy-start.14 = (pred[24]{0:T(512)(128)(4,1)}, pred[24]{0:T(512)(128)(4,1)S(1)}, u32[]{:S(2)}) copy-start(pred[24]{0:T(512)(128)(4,1)S(1)} %get-tuple-element.32) | copy-start | bytes 76
  13.5 77.9 %copy-start.18 = (pred[24]{0:T(512)(128)(4,1)}, pred[24]{0:T(512)(128)(4,1)S(1)}, u32[]{:S(2)}) copy-start(pred[24]{0:T(512)(128)(4,1)S(1)} %get-tuple-element.34) | copy-start | bytes 76
  16.0 143.2 %copy-start.20 = (pred[24]{0:T(512)(128)(4,1)}, pred[24]{0:T(512)(128)(4,1)S(1)}, u32[]{:S(2)}) copy-start(pred[24]{0:T(512)(128)(4,1)S(1)} %get-tuple-element.15) | copy-start | bytes 76
  87.6 0.9 copy-start.2
  162.2 1.8 copy-start.1
  168.4 0.9 copy-start.6
  170.2 0.9 copy-start.16
  171.0 2.1 copy-start.7
  174.1 13.1 %copy-start.11 = (f32[24,32]{1,0:T(8,128)S(1)}, f32[24,32]{1,0:T(8,128)}, u32[]{:S(2)}) copy-start(f32[24,32]{1,0:T(8,128)} %fusion.24) | copy-start | bytes 9220
  202.5 9.1 %copy-start.3 = (bf16[24,128,128]{2,1,0:T(8,128)(2,1)S(1)}, bf16[24,128,128]{2,1,0:T(8,128)(2,1)}, u32[]{:S(2)}) copy-start(bf16[24,128,128]{2,1,0:T(8,128)(2,1)} %copy-done.2) | copy-start | bytes 2359300
  202.5 9.1 %copy-start.13 = (pred[24]{0:T(512)(128)(4,1)S(1)}, pred[24]{0:T(512)(128)(4,1)}, u32[]{:S(2)}) copy-start(pred[24]{0:T(512)(128)(4,1)} %copy-done.12) | copy-start | bytes 76
  202.5 9.1 %copy-start.15 = (pred[24]{0:T(512)(128)(4,1)S(1)}, pred[24]{0:T(512)(128)(4,1)}, u32[]{:S(2)}) copy-start(pred[24]{0:T(512)(128)(4,1)} %copy-done.14) | copy-start | bytes 76
  202.5 147.2 %all-to-all-start = ((bf16[128,32,128]{2,0,1:T(8,128)(2,1)}), bf16[128,32,128]{2,0,1:T(8,128)(2,1)S(1)}, u32[]{:S(2)}, u32[]{:S(2)}) async-start(bf16[128,32,128]{2,0,1:T(8,128)(2,1)} %copy.69), calls=%async_computation | async-start | bytes 2097152 | tf_op jit(solution)/shard_map/all_to_all | solution.py:96
  211.5 2.7 copy-start.4
  211.5 2.7 copy-start.17
  211.5 133.9 %all-reduce.6.cloned.1.call-start = ((), (), s32[]{:S(2)}) async-start(), calls=%async_computation.3 | async-start | bytes 4718592
  211.6 2.7 copy-start.8
  211.6 2.6 copy-start.19
  215.7 1.1 copy-start.5
  215.7 1.1 copy-start.21
  215.7 1.1 copy-start.25
  216.8 1.1 copy-start.9
  216.8 1.1 copy-start.22
  217.4 1.7 copy-start.10
  217.4 1.7 copy-start.23
  218.0 2.2 copy-start.24
Sparse Core Ops, SparseCore 0:
  10.7 74.5 all-gather.4
  87.9 67.8 all-gather.2
  221.5 123.9 all-reduce.5
where the time goes:
time: 358 us; the launch traced here: 357 us
  waiting for transfers between devices  249 us (70%)
  other arithmetic  44.7 us (12%)
  local copies, waits for them, and re-layouts  27.3 us (8%)
  between operations  14.8 us (4%)
  matrix products  11.6 us (3%)
  starting transfers between devices  9.13 us (3%)
    unnamed x4, waiting for transfers between devices  122 us
    all_gather x1, waiting for transfers between devices, on_device(): lax.all_gather(inputs, 'tensor', axis=1, tiled=True)  66.7 us
    all_gather x1, waiting for transfers between devices, on_device(): lax.all_gather(cotangent, 'tensor', axis=1, tiled=True)  60.6 us
    reduce_sum x4, other arithmetic, select_sum(): return jnp.sum(values[:, :, None, :] * table[None, :, :, None], axis=1)  31.7 us
    unnamed x58, local copies, waits for them, and re-layouts  10.7 us
    all_to_all x1, starting transfers between devices, on_device(): lax.all_to_all(pieces, 'tensor', split_axis=1, concat_axis=1, tiled=True)  9 us
  transfers between devices with their start and end apart: 4, of which 3 were waited for; matrix products, arithmetic and copies ran while one was open for 9% of the time, Pallas kernels for 0%

commit v1 on v0

v1 whole, which is shorter than its diff:
```python
import functools
import math

import jax
import jax.numpy as jnp
from jax import lax
from jax.experimental import pallas as pl
from jax.experimental.pallas import tpu as pltpu
from jax.sharding import PartitionSpec as P

BF = jnp.bfloat16
F32 = jnp.float32
NB = 128
HB = 4
DB = 32
NS = 24
NT = 32
NP = 16
UNROLL = 8


def dot(a, b, ca, cb):
    return lax.dot_general(a, b, (((ca,), (cb,)), ((), ())), preferred_element_type=F32)


def slots(body):
    def some(i, carry):
        for u in range(UNROLL):
            body(i * UNROLL + u)
        return carry

    lax.fori_loop(0, NS // UNROLL, some, 0)


def feature(e):
    return lax.shift_right_logical(jnp.maximum(e, 0), 2)


def row(e):
    return jnp.maximum(e, 0) & (HB - 1)


def place(e, z, core):
    d = feature(e)
    rel = (lax.shift_right_logical(d, 1) - z) & 15
    group = (d & 1) ^ core
    lane = rel & 3
    step = lax.shift_right_logical(rel, 2)
    step = jnp.where(lane == 3, (step + 1) & 3, step)
    return jnp.where(e >= 0, group * 16 + lane * 4 + step, DB)


def forward_kernel(gl, ul, dl, here, acts, gw, uw, dw, p_own, p_other, gg_ref, gu_ref, hid_ref, prods, acc, accp):
    z, core = here[0], here[1]
    acc[...] = jnp.zeros_like(acc)
    accp[...] = jnp.zeros_like(accp)

    def project(which, entries, side, weights, contract):
        def multiply(k):
            prods[k] = dot(acts[feature(entries[0, k]), side], weights[0, k], 1, contract)

        def add(k):
            e = entries[0, k]
            r = jnp.where(e >= 0, row(e), HB)
            acc[which, r] += prods[k]

        slots(multiply)
        slots(add)

    project(0, gl, 0, gw, 0)
    project(1, ul, 0, uw, 0)
    project(2, dl, 1, dw, 1)
    for r in range(HB):
        gate, up, gh = acc[0, r], acc[1, r], acc[2, r]
        sig = jax.nn.sigmoid(gate)
        act = gate * sig
        hid_ref[r] = (act * up).astype(BF)
        gg_ref[r] = (gh * up * sig * (1.0 + gate * (1.0 - sig))).astype(BF)
        gu_ref[r] = (gh * act).astype(BF)

    def back(entries, grads, weights):
        def multiply(k):
            prods[k] = dot(grads[row(entries[0, k])], weights[0, k], 1, 1)

        def add(k):
            accp[place(entries[0, k], z, core)] += prods[k]

        slots(multiply)
        slots(add)

    back(gl, gg_ref, gw)
    back(ul, gu_ref, uw)
    for i in range(16):
        p_own[i] = accp[i].astype(BF)
        p_other[i] = accp[16 + i].astype(BF)


def terms_kernel(gl, ul, dl, acts, gg, gu, hid, out, *, scale):
    def write(slot, e, product):
        live = jnp.where(e >= 0, scale, 0.0)
        out[:, slot] = (product * live).astype(BF).reshape(NP, NB // NP, NB)

    def gate(k):
        e = gl[0, k]
        write(k, e, dot(acts[feature(e), 0], gg[row(e)], 0, 0))

    def up(k):
        e = ul[0, k]
        write(NS + k, e, dot(acts[feature(e), 0], gu[row(e)], 0, 0))

    def down(k):
        e = dl[0, k]
        write(2 * NS + k, e, dot(hid[row(e)], acts[feature(e), 1], 0, 0))

    slots(gate)
    slots(up)
    slots(down)


SMEM = pl.BlockSpec(memory_space=pltpu.SMEM)
VMEM = pl.BlockSpec(memory_space=pltpu.VMEM)


def forward(lists, here, acts, weights):
    block = jax.ShapeDtypeStruct((HB, NB, NB), BF)
    half = jax.ShapeDtypeStruct((16, NB, NB), BF)
    return pl.pallas_call(
        forward_kernel,
        in_specs=[SMEM] * 4 + [VMEM] * 4,
        out_specs=[VMEM] * 5,
        out_shape=[half, half, block, block, block],
        scratch_shapes=[
            pltpu.VMEM((NS, NB, NB), F32),
            pltpu.VMEM((3, HB + 1, NB, NB), F32),
            pltpu.VMEM((DB + 1, NB, NB), F32),
        ],
        compiler_params=pltpu.CompilerParams(vmem_limit_bytes=24 << 20),
        name="forward_backward",
    )(*lists, here, acts, *weights)


def weight_terms(lists, acts, gg, gu, hid, scale):
    return pl.pallas_call(
        functools.partial(terms_kernel, scale=scale),
        in_specs=[SMEM] * 3 + [VMEM] * 4,
        out_specs=VMEM,
        out_shape=jax.ShapeDtypeStruct((NP, 3 * NS, NB // NP, NB), BF),
        compiler_params=pltpu.CompilerParams(vmem_limit_bytes=16 << 20),
        name="weight_terms",
    )(*lists, acts, gg, gu, hid)


def shift(x, steps):
    return lax.ppermute(x, "tensor", [(i, (i + 2 * steps) % NT) for i in range(NT)])


def swap(x):
    return lax.ppermute(x, "tensor", [(i, i ^ 1) for i in range(NT)])


def total(*parts):
    return functools.reduce(jnp.add, [p.astype(F32) for p in parts]).astype(BF)


def reduce_features(p_own, p_other):
    s = total(p_own, swap(p_other)).reshape(4, 4, NB, NB)
    from_left = shift(s[1], 1)
    from_right = shift(s[3], -1)
    from_left2 = shift(s[2, :2], 2)
    from_right2 = shift(s[2, 2:], -2)
    u = [
        total(s[0, 0], from_left[0], from_right[0], from_left2[0], from_right2[1]),
        total(s[0, 1], from_left[1], from_right[1], from_left2[1]),
        total(s[0, 2], from_left[2], from_right[2]),
        total(s[0, 3], from_left[3], from_right[3], from_right2[0]),
    ]
    return total(u[0], shift(u[1], 4), shift(u[2], 8), shift(u[3], -4))


def on_device(inputs, cotangent, gate_w, up_w, down_w, gate_list, up_list, down_list):
    scale = 1.0 / math.sqrt(inputs.shape[0] * NP)
    me = lax.axis_index("tensor")
    here = jnp.stack([me // 2, me % 2]).astype(jnp.int32)
    lists = (gate_list, up_list, down_list)
    acts = lax.all_gather(jnp.stack([inputs, cotangent]), "tensor", axis=0)
    p_own, p_other, gg, gu, hid = forward(lists, here, acts, (gate_w, up_w, down_w))
    terms = weight_terms(lists, acts, gg, gu, hid, scale)
    got = lax.all_to_all(terms, "dp", 0, 0, tiled=True)
    grad_x = reduce_features(p_own, p_other)
    grads = jnp.sum(got.astype(F32), axis=0).astype(BF)
    return grad_x, grads[None, :NS], grads[None, NS : 2 * NS], grads[None, 2 * NS :]


def solution(mesh):
    w4, l2 = P("tensor", None, None, None), P("tensor", None)
    scattered = P("tensor", None, "dp", None)
    return jax.shard_map(
        on_device,
        mesh=mesh,
        in_specs=(P("dp", "tensor"), P("dp", "tensor"), w4, w4, w4, l2, l2, l2),
        out_specs=(P("dp", "tensor"), scattered, scattered, scattered),
        check_vma=False,
    )
```

time: 358 us -> 165 us (0.46)
  the two profiles are of different devices: /device:TPU:32 before, /device:TPU:66 now
where the time goes in v1:
time: 165 us; the launch traced here: 164 us
  waiting for transfers between devices  89.9 us (54%)
  starting transfers between devices  39 us (24%)
  between operations  14.2 us (9%)
  Pallas kernels  10.5 us (6%)
  local copies, waits for them, and re-layouts  7.64 us (5%)
  other arithmetic  2.66 us (2%)
    all_gather x1, waiting for transfers between devices, on_device(): acts = lax.all_gather(jnp.stack([inputs, cotangent]), 'tensor', axis=0)  75.5 us
    ppermute x7, starting transfers between devices, shift(): lax.ppermute(x, 'tensor', [(i, (i + 2 * steps) % NT) for i in range(NT)])  29.8 us
    ppermute x7, waiting for transfers between devices, shift(): lax.ppermute(x, 'tensor', [(i, (i + 2 * steps) % NT) for i in range(NT)])  12.5 us
    all_to_all x1, starting transfers between devices, on_device(): got = lax.all_to_all(terms, 'dp', 0, 0, tiled=True)  7.31 us
    unnamed x14, local copies, waits for them, and re-layouts  6.95 us
    pallas_call x1, Pallas kernels, forward(): pl.pallas_call(forward_kernel, in_specs=[SMEM] * 4 + [VMEM] * 4, out_spec...  6.12 us
    pallas_call x1, Pallas kernels, weight_terms(): pl.pallas_call(functools.partial(terms_kernel, scale=scale), in_specs=[SM...  4.42 us
  transfers between devices with their start and end apart: 10, of which 6 were waited for; matrix products, arithmetic and copies ran while one was open for 1% of the time, Pallas kernels for 0%

profile of v1, /device:TPU:66, one launch (start us, length us, event | category | flops | bytes accessed | tf_op | source)
XLA Modules:
  0.0 164.0 jit_solution(3971455896884473404)
XLA Ops:
  7.2 0.0 all-gather.3.cloned.1.call-start
  7.2 1.4 pad_maximum_fusion
  8.7 0.1 pad_add_fusion.here
  8.7 75.5 %all-gather.3.cloned.1.call-done = bf16[64,128,128]{2,1,0:T(8,128)(2,1)} async-done(((bf16[2,128,128]{2,1,0:T(8,128)(2,1)}), bf16[64,128,128]{2,1,0:T(8,128)(2,1)}) %all-gather.3.cloned.1.call-update) | async-done | bytes 2097168 | tf_op jit(solution)/shard_map/all_gather | solution.py:185
  84.3 1.6 copy-done
  85.9 1.1 copy-done.1
  87.0 1.1 copy-done.2
  88.1 1.1 copy-done.3
  89.3 0.7 copy-done.4
  89.9 0.7 copy-done.5
  90.6 0.7 copy-done.6
  91.2 6.1 %forward_backward.1 = (bf16[16,128,128]{2,1,0:T(8,128)(2,1)S(1)}, bf16[16,128,128]{2,1,0:T(8,128)(2,1)S(1)}, bf16[4,128,128]{2,1,0:T(8,128)(2,1)S(1)}, bf16[4,12...) custom-call(s32[1,24]{1,0:T(1,128)S(1)} %copy-done.4, s32[1,24]{1,0:T(1,128)S(1)} %copy-done.5, s32[1,24]{1,0:T(1,128)S(1)} %copy-done.6, ...), custom_call_target="tpu_custom_call" | custom-call | tf_op jit(solution)/shard_map/forward_backward/pallas_call | solution.py:127
  97.4 4.4 %weight_terms.1 = bf16[16,72,8,128]{3,2,1,0:T(8,128)(2,1)} custom-call(s32[1,24]{1,0:T(1,128)S(1)} %copy-done.4, s32[1,24]{1,0:T(1,128)S(1)} %copy-done.5, s32[1,24]{1,0:T(1,128)S(1)} %copy-done.6, bf16[32,2,128,128]{3,2,1,0:T(8,128)(2,1)S(1)} %bitcast.97, bf16[4,128,128]{2,1,0:T(8,128)(2,1)S(1)} %get-tuple-element.11.gg, ...), custom_call_target="tpu_custom_call" | custom-call | tf_op jit(solution)/shard_map/weight_terms/pallas_call | solution.py:143
  101.8 7.3 %all-to-all-start = ((bf16[16,72,8,128]{3,2,1,0:T(8,128)(2,1)}), bf16[16,72,8,128]{3,2,1,0:T(8,128)(2,1)S(1)}, u32[]{:S(2)}, u32[]{:S(2)}) async-start(bf16[16,72,8,128]{3,2,1,0:T(8,128)(2,1)} %weight_terms.1), calls=%async_computation | async-start | bytes 4718592 | tf_op jit(solution)/shard_map/all_to_all | solution.py:188
  109.1 1.9 %collective-permute-start = (bf16[16,128,128]{2,1,0:T(8,128)(2,1)S(1)}, bf16[16,128,128]{2,1,0:T(8,128)(2,1)S(1)}, u32[]{:S(2)}, u32[]{:S(2)}) collective-permute-start(bf16[16,128,128]{2,1,0:T(8,128)(2,1)S(1)} %get-tuple-element.10), channel_id=1, source_target_pairs={{0,1},{1,0},{2,3},{3,2},{4,5},{5,4},{6,7},{7,6},{8,9},{9,8},{10,11... | collective-permute-start | bytes 1572872 | tf_op jit(solution)/shard_map/ppermute | solution.py:158
  111.0 1.9 %collective-permute-done = bf16[16,128,128]{2,1,0:T(8,128)(2,1)S(1)} collective-permute-done((bf16[16,128,128]{2,1,0:T(8,128)(2,1)S(1)}, bf16[16,128,128]{2,1,0:T(8,128)(2,1)S(1)}, u32[]{:S(2)}, u32[]{:S(2)}) %collective-permute-start) | collective-permute-done | bytes 524320 | tf_op jit(solution)/shard_map/ppermute | solution.py:158
  112.9 0.1 add_convert_fusion
  113.0 3.4 %collective-permute-start.2 = (bf16[4,128,128]{2,1,0:T(8,128)(2,1)S(1)}, bf16[4,128,128]{2,1,0:T(8,128)(2,1)S(1)}, u32[]{:S(2)}, u32[]{:S(2)}) collective-permute-start(bf16[4,128,128]{2,1,0:T(8,128)(2,1)S(1)} %get-tuple-element.20), channel_id=1, source_target_pairs={{0,30},{1,31},{2,0},{3,1},{4,2},{5,3},{6,4},{7,5},{8,6},{9,7},{10,... | collective-permute-start | bytes 393224 | tf_op jit(solution)/shard_map/ppermute | solution.py:154
  116.5 2.4 %collective-permute-start.1 = (bf16[4,128,128]{2,1,0:T(8,128)(2,1)S(1)}, bf16[4,128,128]{2,1,0:T(8,128)(2,1)S(1)}, u32[]{:S(2)}, u32[]{:S(2)}) collective-permute-start(bf16[4,128,128]{2,1,0:T(8,128)(2,1)S(1)} %get-tuple-element.19), channel_id=1, source_target_pairs={{0,2},{1,3},{2,4},{3,5},{4,6},{5,7},{6,8},{7,9},{8,10},{9,11},{10,... | collective-permute-start | bytes 393224 | tf_op jit(solution)/shard_map/ppermute | solution.py:154
  118.9 3.9 %collective-permute-start.3 = (bf16[2,128,128]{2,1,0:T(8,128)(2,1)S(1)}, bf16[2,128,128]{2,1,0:T(8,128)(2,1)S(1)}, u32[]{:S(2)}, u32[]{:S(2)}) collective-permute-start(bf16[2,128,128]{2,1,0:T(8,128)(2,1)S(1)} %get-tuple-element.17), channel_id=1, source_target_pairs={{0,4},{1,5},{2,6},{3,7},{4,8},{5,9},{6,10},{7,11},{8,12},{9,13},{1... | collective-permute-start | bytes 196616 | tf_op jit(solution)/shard_map/ppermute | solution.py:154
  122.8 2.9 %collective-permute-start.4 = (bf16[2,128,128]{2,1,0:T(8,128)(2,1)S(1)}, bf16[2,128,128]{2,1,0:T(8,128)(2,1)S(1)}, u32[]{:S(2)}, u32[]{:S(2)}) collective-permute-start(bf16[2,128,128]{2,1,0:T(8,128)(2,1)S(1)} %get-tuple-element.18), channel_id=1, source_target_pairs={{0,28},{1,29},{2,30},{3,31},{4,0},{5,1},{6,2},{7,3},{8,4},{9,5},{1... | collective-permute-start | bytes 196616 | tf_op jit(solution)/shard_map/ppermute | solution.py:154
  125.7 0.4 collective-permute-done.3
  126.1 5.2 %collective-permute-done.4 = bf16[2,128,128]{2,1,0:T(8,128)(2,1)S(1)} collective-permute-done((bf16[2,128,128]{2,1,0:T(8,128)(2,1)S(1)}, bf16[2,128,128]{2,1,0:T(8,128)(2,1)S(1)}, u32[]{:S(2)}, u32[]{:S(2)}) %collective-permute-start.4) | collective-permute-done | bytes 65568 | tf_op jit(solution)/shard_map/ppermute | solution.py:154
  131.2 0.1 fusion.2
  131.3 6.3 %collective-permute-start.7 = (bf16[128,128]{1,0:T(8,128)(2,1)S(1)}, bf16[128,128]{1,0:T(8,128)(2,1)S(1)}, u32[]{:S(2)}, u32[]{:S(2)}) collective-permute-start(bf16[128,128]{1,0:T(8,128)(2,1)S(1)} %get-tuple-element.15), channel_id=1, source_target_pairs={{0,24},{1,25},{2,26},{3,27},{4,28},{5,29},{6,30},{7,31},{8,0},{9,1... | collective-permute-start | bytes 98312 | tf_op jit(solution)/shard_map/ppermute | solution.py:154
  137.5 7.5 %collective-permute-start.6 = (bf16[128,128]{1,0:T(8,128)(2,1)S(1)}, bf16[128,128]{1,0:T(8,128)(2,1)S(1)}, u32[]{:S(2)}, u32[]{:S(2)}) collective-permute-start(bf16[128,128]{1,0:T(8,128)(2,1)S(1)} %get-tuple-element.16), channel_id=1, source_target_pairs={{0,16},{1,17},{2,18},{3,19},{4,20},{5,21},{6,22},{7,23},{8,24},{9,... | collective-permute-start | bytes 98312 | tf_op jit(solution)/shard_map/ppermute | solution.py:154
  145.1 3.4 %collective-permute-start.5 = (bf16[128,128]{1,0:T(8,128)(2,1)S(1)}, bf16[128,128]{1,0:T(8,128)(2,1)S(1)}, u32[]{:S(2)}, u32[]{:S(2)}) collective-permute-start(bf16[128,128]{1,0:T(8,128)(2,1)S(1)} %get-tuple-element.14), channel_id=1, source_target_pairs={{0,8},{1,9},{2,10},{3,11},{4,12},{5,13},{6,14},{7,15},{8,16},{9,17... | collective-permute-start | bytes 98312 | tf_op jit(solution)/shard_map/ppermute | solution.py:154
  148.5 3.6 %collective-permute-done.6 = bf16[128,128]{1,0:T(8,128)(2,1)S(1)} collective-permute-done((bf16[128,128]{1,0:T(8,128)(2,1)S(1)}, bf16[128,128]{1,0:T(8,128)(2,1)S(1)}, u32[]{:S(2)}, u32[]{:S(2)}) %collective-permute-start.6) | collective-permute-done | bytes 32800 | tf_op jit(solution)/shard_map/ppermute | solution.py:154
  152.1 3.3 %collective-permute-done.5 = bf16[128,128]{1,0:T(8,128)(2,1)S(1)} collective-permute-done((bf16[128,128]{1,0:T(8,128)(2,1)S(1)}, bf16[128,128]{1,0:T(8,128)(2,1)S(1)}, u32[]{:S(2)}, u32[]{:S(2)}) %collective-permute-start.5) | collective-permute-done | bytes 32800 | tf_op jit(solution)/shard_map/ppermute | solution.py:154
  155.5 0.7 add_convert_fusion.1
  156.1 0.3 reduce_sum.12
  156.5 0.7 slice_bitcast_fusion.2
  (14 shorter events, 0.1 us)
Async XLA Ops:
  7.2 77.1 %all-gather.3.cloned.1.call-start = ((), (), s32[]{:S(2)}) async-start(), calls=%async_computation.1 | async-start | bytes 2162688 | tf_op jit(solution)/shard_map/all_gather | solution.py:185
  84.3 1.6 copy-start
  85.9 1.1 copy-start.1
  87.0 1.1 copy-start.2
  88.1 1.1 copy-start.3
  89.3 0.7 copy-start.4
  89.9 0.7 copy-start.5
  90.6 0.7 copy-start.6
  101.8 54.4 %all-to-all-start = ((bf16[16,72,8,128]{3,2,1,0:T(8,128)(2,1)}), bf16[16,72,8,128]{3,2,1,0:T(8,128)(2,1)S(1)}, u32[]{:S(2)}, u32[]{:S(2)}) async-start(bf16[16,72,8,128]{3,2,1,0:T(8,128)(2,1)} %weight_terms.1), calls=%async_computation | async-start | bytes 4718592 | tf_op jit(solution)/shard_map/all_to_all | solution.py:188
  109.1 3.8 %collective-permute-start = (bf16[16,128,128]{2,1,0:T(8,128)(2,1)S(1)}, bf16[16,128,128]{2,1,0:T(8,128)(2,1)S(1)}, u32[]{:S(2)}, u32[]{:S(2)}) collective-permute-start(bf16[16,128,128]{2,1,0:T(8,128)(2,1)S(1)} %get-tuple-element.10), channel_id=1, source_target_pairs={{0,1},{1,0},{2,3},{3,2},{4,5},{5,4},{6,7},{7,6},{8,9},{9,8},{10,11... | collective-permute-start | bytes 1572872 | tf_op jit(solution)/shard_map/ppermute | solution.py:158
  113.0 18.2 %collective-permute-start.2 = (bf16[4,128,128]{2,1,0:T(8,128)(2,1)S(1)}, bf16[4,128,128]{2,1,0:T(8,128)(2,1)S(1)}, u32[]{:S(2)}, u32[]{:S(2)}) collective-permute-start(bf16[4,128,128]{2,1,0:T(8,128)(2,1)S(1)} %get-tuple-element.20), channel_id=1, source_target_pairs={{0,30},{1,31},{2,0},{3,1},{4,2},{5,3},{6,4},{7,5},{8,6},{9,7},{10,... | collective-permute-start | bytes 393224 | tf_op jit(solution)/shard_map/ppermute | solution.py:154
  116.5 14.7 %collective-permute-start.1 = (bf16[4,128,128]{2,1,0:T(8,128)(2,1)S(1)}, bf16[4,128,128]{2,1,0:T(8,128)(2,1)S(1)}, u32[]{:S(2)}, u32[]{:S(2)}) collective-permute-start(bf16[4,128,128]{2,1,0:T(8,128)(2,1)S(1)} %get-tuple-element.19), channel_id=1, source_target_pairs={{0,2},{1,3},{2,4},{3,5},{4,6},{5,7},{6,8},{7,9},{8,10},{9,11},{10,... | collective-permute-start | bytes 393224 | tf_op jit(solution)/shard_map/ppermute | solution.py:154
  118.9 7.1 %collective-permute-start.3 = (bf16[2,128,128]{2,1,0:T(8,128)(2,1)S(1)}, bf16[2,128,128]{2,1,0:T(8,128)(2,1)S(1)}, u32[]{:S(2)}, u32[]{:S(2)}) collective-permute-start(bf16[2,128,128]{2,1,0:T(8,128)(2,1)S(1)} %get-tuple-element.17), channel_id=1, source_target_pairs={{0,4},{1,5},{2,6},{3,7},{4,8},{5,9},{6,10},{7,11},{8,12},{9,13},{1... | collective-permute-start | bytes 196616 | tf_op jit(solution)/shard_map/ppermute | solution.py:154
  122.8 8.4 %collective-permute-start.4 = (bf16[2,128,128]{2,1,0:T(8,128)(2,1)S(1)}, bf16[2,128,128]{2,1,0:T(8,128)(2,1)S(1)}, u32[]{:S(2)}, u32[]{:S(2)}) collective-permute-start(bf16[2,128,128]{2,1,0:T(8,128)(2,1)S(1)} %get-tuple-element.18), channel_id=1, source_target_pairs={{0,28},{1,29},{2,30},{3,31},{4,0},{5,1},{6,2},{7,3},{8,4},{9,5},{1... | collective-permute-start | bytes 196616 | tf_op jit(solution)/shard_map/ppermute | solution.py:154
  131.3 17.2 %collective-permute-start.7 = (bf16[128,128]{1,0:T(8,128)(2,1)S(1)}, bf16[128,128]{1,0:T(8,128)(2,1)S(1)}, u32[]{:S(2)}, u32[]{:S(2)}) collective-permute-start(bf16[128,128]{1,0:T(8,128)(2,1)S(1)} %get-tuple-element.15), channel_id=1, source_target_pairs={{0,24},{1,25},{2,26},{3,27},{4,28},{5,29},{6,30},{7,31},{8,0},{9,1... | collective-permute-start | bytes 98312 | tf_op jit(solution)/shard_map/ppermute | solution.py:154
  137.5 14.6 %collective-permute-start.6 = (bf16[128,128]{1,0:T(8,128)(2,1)S(1)}, bf16[128,128]{1,0:T(8,128)(2,1)S(1)}, u32[]{:S(2)}, u32[]{:S(2)}) collective-permute-start(bf16[128,128]{1,0:T(8,128)(2,1)S(1)} %get-tuple-element.16), channel_id=1, source_target_pairs={{0,16},{1,17},{2,18},{3,19},{4,20},{5,21},{6,22},{7,23},{8,24},{9,... | collective-permute-start | bytes 98312 | tf_op jit(solution)/shard_map/ppermute | solution.py:154
  145.1 10.4 %collective-permute-start.5 = (bf16[128,128]{1,0:T(8,128)(2,1)S(1)}, bf16[128,128]{1,0:T(8,128)(2,1)S(1)}, u32[]{:S(2)}, u32[]{:S(2)}) collective-permute-start(bf16[128,128]{1,0:T(8,128)(2,1)S(1)} %get-tuple-element.14), channel_id=1, source_target_pairs={{0,8},{1,9},{2,10},{3,11},{4,12},{5,13},{6,14},{7,15},{8,16},{9,17... | collective-permute-start | bytes 98312 | tf_op jit(solution)/shard_map/ppermute | solution.py:154
Sparse Core Ops, SparseCore 0:
  10.1 74.1 all-gather.2

commit v2 on v1

v2 whole, which is shorter than its diff:
```python
import functools
import math

import jax
import jax.numpy as jnp
from jax import lax
from jax.experimental import pallas as pl
from jax.experimental.pallas import tpu as pltpu
from jax.sharding import PartitionSpec as P


BF = jnp.bfloat16
F32 = jnp.float32
NB = 128
HB = 4
DB = 32
NS = 24
NT = 32
NP = 16
UNROLL = 24
NZ = 16
FAR = (0, 5, -5)
NEAR = (1, 2)
OPPOSITE = 8


def dot(a, b, ca, cb):
    return lax.dot_general(a, b, (((ca,), (cb,)), ((), ())), preferred_element_type=F32)


def slots(body):
    def some(i, carry):
        for u in range(UNROLL):
            body(i * UNROLL + u)
        return carry

    lax.fori_loop(0, NS // UNROLL, some, 0)


def feature(e):
    return lax.shift_right_logical(jnp.maximum(e, 0), 2)


def row(e):
    return jnp.maximum(e, 0) & (HB - 1)


def orders(core):
    held, sent = {}, {}
    for other in range(2):
        for f, far in enumerate(FAR):
            held[other * NZ + far % NZ] = other * 3 + f
            sent[other * NZ + far % NZ] = other * 16 + 12 + f
            for n, near in enumerate(NEAR):
                for way in (1, -1):
                    at = other * NZ + (way * near + far) % NZ
                    mine = (way == 1) == (core == 0)
                    held[at] = 19 + n * 6 + (1 - other) * 3 + f if mine else 6 + n * 6 + other * 3 + f
                    sent[at] = n * 6 + other * 3 + f if mine else 16 + n * 6 + (1 - other) * 3 + f
        held[other * NZ + OPPOSITE] = 31 if other else 18
        sent[other * NZ + OPPOSITE] = 31 if other else 15
    for table in (held, sent):
        assert sorted(table) == sorted(table.values()) == list(range(2 * NZ))
    return [held[i] for i in range(2 * NZ)] + [sent[i] for i in range(2 * NZ)]


def place(e, here, table):
    d = feature(e)
    offset = (lax.shift_right_logical(d, 1) - here[0]) & (NZ - 1)
    return here[2 + table * 2 * NZ + ((d & 1) ^ here[1]) * NZ + offset]


def forward_kernel(gl, ul, dl, here, far, far_s, near, near_s, gw, uw, dw, p_own, p_other, gg_ref, gu_ref, hid_ref, acts, acc, accp, weights, sems):
    loads = []
    for src, start, size in (
        (far, 0, 3),
        (far_s, 3, 3),
        (near, 6, 13),
        (near_s, 19, 13),
    ):
        loads.append(pltpu.make_async_copy(src, acts.at[pl.ds(start, size)], sems.at[len(loads)]))
    for src, dst in (
        (gw.at[0], weights.at[0]),
        (uw.at[0], weights.at[1]),
        (dw.at[0], weights.at[2]),
    ):
        loads.append(pltpu.make_async_copy(src, dst, sems.at[len(loads)]))
    for load in loads:
        load.start()
    acc[...] = jnp.zeros_like(acc)
    accp[...] = jnp.zeros_like(accp)
    for load in loads[:4]:
        load.wait()

    def project(which, entries, side, contract):
        loads[4 + which].wait()

        def add(k):
            e = entries[0, k]
            r = jnp.where(e >= 0, row(e), HB)
            acc[which, r] += dot(acts[place(e, here, 0), side], weights[which, k], 1, contract)

        slots(add)

    project(0, gl, 0, 0)
    project(1, ul, 0, 0)
    project(2, dl, 1, 1)
    for r in range(HB):
        gate, up, gh = acc[0, r], acc[1, r], acc[2, r]
        sig = jax.nn.sigmoid(gate)
        act = gate * sig
        hid_ref[r] = (act * up).astype(BF)
        gg_ref[r] = (gh * up * sig * (1.0 + gate * (1.0 - sig))).astype(BF)
        gu_ref[r] = (gh * act).astype(BF)

    def back(entries, grads, which):
        def add(k):
            e = entries[0, k]
            accp[jnp.where(e >= 0, place(e, here, 1), DB)] += dot(grads[row(e)], weights[which, k], 1, 1)

        slots(add)

    back(gl, gg_ref, 0)
    back(ul, gu_ref, 1)
    for i in range(16):
        p_own[i] = accp[i].astype(BF)
        p_other[i] = accp[16 + i].astype(BF)


def terms_kernel(gl, ul, dl, here, acts, gg, gu, hid, out, *, scale):
    def write(slot, e, product):
        live = jnp.where(e >= 0, scale, 0.0)
        out[:, slot] = (product * live).astype(BF).reshape(NP, NB // NP, NB)

    def gate(k):
        e = gl[0, k]
        write(k, e, dot(acts[place(e, here, 0), 0], gg[row(e)], 0, 0))

    def up(k):
        e = ul[0, k]
        write(NS + k, e, dot(acts[place(e, here, 0), 0], gu[row(e)], 0, 0))

    def down(k):
        e = dl[0, k]
        write(2 * NS + k, e, dot(hid[row(e)], acts[place(e, here, 0), 1], 0, 0))

    slots(gate)
    slots(up)
    slots(down)


SMEM = pl.BlockSpec(memory_space=pltpu.SMEM)
VMEM = pl.BlockSpec(memory_space=pltpu.VMEM)
ANY = pl.BlockSpec(memory_space=pl.ANY)
HBM = pl.BlockSpec(memory_space=pltpu.HBM)


def forward(lists, here, acts, weights):
    block = jax.ShapeDtypeStruct((HB, NB, NB), BF)
    half = jax.ShapeDtypeStruct((16, NB, NB), BF)
    return pl.pallas_call(
        forward_kernel,
        in_specs=[SMEM] * 4 + [ANY] * 4 + [HBM] * 3,
        out_specs=[VMEM] * 6,
        out_shape=[half, half, block, block, block, jax.ShapeDtypeStruct((DB, 2, NB, NB), BF)],
        scratch_shapes=[
            pltpu.VMEM((3, HB + 1, NB, NB), F32),
            pltpu.VMEM((DB + 1, NB, NB), F32),
            pltpu.VMEM((3, NS, NB, NB), BF),
            pltpu.SemaphoreType.DMA((7,)),
        ],
        compiler_params=pltpu.CompilerParams(vmem_limit_bytes=44 << 20),
        name="forward_backward",
    )(*lists, here, *acts, *weights)


def weight_terms(lists, here, acts, gg, gu, hid, scale):
    return pl.pallas_call(
        functools.partial(terms_kernel, scale=scale),
        in_specs=[SMEM] * 4 + [VMEM] * 4,
        out_specs=VMEM,
        out_shape=jax.ShapeDtypeStruct((NP, 3 * NS, NB // NP, NB), BF),
        compiler_params=pltpu.CompilerParams(vmem_limit_bytes=6 << 20),
        name="weight_terms",
    )(*lists, here, acts, gg, gu, hid)


def shift(x, steps):
    return lax.ppermute(x, "tensor", [(i, (i + 2 * steps) % NT) for i in range(NT)])


def swap(x):
    return lax.ppermute(x, "tensor", [(i, i ^ 1) for i in range(NT)])


def total(*parts):
    return functools.reduce(jnp.add, [p.astype(F32) for p in parts]).astype(BF)


def part_ways(x, steps):
    return lax.ppermute(x, "tensor", [(i, (i + (2 * steps if i % 2 == 0 else -2 * steps)) % NT) for i in range(NT)])


def reduce_features(p_own, p_other):
    p_other = swap(p_other)
    s = total(p_own, p_other)
    r1 = part_ways(s[:6], NEAR[0])
    r2 = part_ways(s[6:12], NEAR[1])
    r3 = shift(s[15], OPPOSITE - FAR[1])
    t = [total(s[12], r1[0], r2[0]), total(s[13], r1[1], r2[1], r3), total(s[14], r1[2], r2[2])]
    t_other = swap(total(r1[3:], r2[3:]))
    u = [total(t[f], t_other[f]) for f in range(3)]
    return total(u[0], shift(u[1], FAR[1]), shift(u[2], FAR[2]))


def gather_features(x):
    far = jnp.stack([x, shift(x, -FAR[1]), shift(x, -FAR[2])])
    far_s = swap(far)
    full = jnp.concatenate([far, far_s])
    one = part_ways(full, NEAR[0])
    two = part_ways(full, NEAR[1])
    last = shift(far[1], FAR[1] - OPPOSITE)[None]
    near = jnp.concatenate([one, two, last])
    return far, far_s, near, swap(near)


def on_device(inputs, cotangent, gate_w, up_w, down_w, gate_list, up_list, down_list):
    scale = 1.0 / math.sqrt(inputs.shape[0] * NP)
    me = lax.axis_index("tensor")
    tables = jnp.array([orders(0), orders(1)], jnp.int32)
    here = jnp.concatenate([jnp.stack([me // 2, me % 2]).astype(jnp.int32), tables[me % 2]])
    lists = (gate_list, up_list, down_list)
    pieces = gather_features(jnp.stack([inputs, cotangent]))
    p_own, p_other, gg, gu, hid, acts = forward(lists, here, pieces, [pltpu.with_memory_space_constraint(w, pltpu.HBM) for w in (gate_w, up_w, down_w)])
    terms = weight_terms(lists, here, acts, gg, gu, hid, scale)
    got = lax.all_to_all(terms, "dp", 0, 0, tiled=True)
    grad_x = reduce_features(p_own, p_other)
    grads = jnp.sum(got.astype(F32), axis=0).astype(BF)
    return grad_x, grads[None, :NS], grads[None, NS : 2 * NS], grads[None, 2 * NS :]


def solution(mesh):
    w4, l2 = P("tensor", None, None, None), P("tensor", None)
    scattered = P("tensor", None, "dp", None)
    return jax.shard_map(
        on_device,
        mesh=mesh,
        in_specs=(P("dp", "tensor"), P("dp", "tensor"), w4, w4, w4, l2, l2, l2),
        out_specs=(P("dp", "tensor"), scattered, scattered, scattered),
        check_vma=False,
    )
```

time: 165 us -> 121 us (0.73)
  the two profiles are of different devices: /device:TPU:66 before, /device:TPU:2 now
where the time goes in v2:
time: 121 us
  starting transfers between devices  64.8 us (54%)
  waiting for transfers between devices  41.6 us (34%)
  Pallas kernels  8.86 us (7%)
  other arithmetic  3.93 us (3%)
    ppermute x6, starting transfers between devices, shift(): lax.ppermute(x, 'tensor', [(i, (i + 2 * steps) % NT) for i in range(NT)])  36.7 us
    ppermute x6, waiting for transfers between devices, shift(): lax.ppermute(x, 'tensor', [(i, (i + 2 * steps) % NT) for i in range(NT)])  29.6 us
    ppermute x4, starting transfers between devices, swap(): return lax.ppermute(x, 'tensor', [(i, i ^ 1) for i in range(NT)])  12 us
    ppermute x4, waiting for transfers between devices, part_ways(): lax.ppermute(x, 'tensor', [(i, (i + (2 * steps if i % 2 == 0 else -2 * st...  8.72 us
    ppermute x4, starting transfers between devices, part_ways(): lax.ppermute(x, 'tensor', [(i, (i + (2 * steps if i % 2 == 0 else -2 * st...  8.67 us
    all_to_all x1, starting transfers between devices, on_device(): got = lax.all_to_all(terms, 'dp', 0, 0, tiled=True)  7.48 us
    pallas_call x1, Pallas kernels, forward(): pl.pallas_call(forward_kernel, in_specs=[SMEM] * 4 + [ANY] * 4 + [HBM] *...  5.98 us
    ppermute x4, waiting for transfers between devices, swap(): return lax.ppermute(x, 'tensor', [(i, i ^ 1) for i in range(NT)])  3.27 us
  transfers between devices with their start and end apart: 15, of which 11 were waited for; matrix products, arithmetic and copies ran while one was open for 1% of the time, Pallas kernels for 2%

profile of v2, /device:TPU:2, one launch (start us, length us, event | category | flops | bytes accessed | tf_op | source)
XLA Modules:
  0.0 120.8 jit_solution(324749375791723017)
XLA Ops:
  0.7 0.8 fusion.6
  1.5 14.4 %collective-permute-start = (bf16[2,128,128]{2,1,0:T(8,128)(2,1)S(1)}, bf16[2,128,128]{2,1,0:T(8,128)(2,1)S(1)}, u32[]{:S(2)}, u32[]{:S(2)}) collective-permute-start(bf16[2,128,128]{2,1,0:T(8,128)(2,1)S(1)} %get-tuple-element.22), channel_id=1, source_target_pairs={{0,22},{1,23},{2,24},{3,25},{4,26},{5,27},{6,28},{7,29},{8,30},{9,... | collective-permute-start | bytes 196616 | tf_op jit(solution)/shard_map/ppermute | solution.py:189
  15.9 1.9 %collective-permute-start.1 = (bf16[2,128,128]{2,1,0:T(8,128)(2,1)S(1)}, bf16[2,128,128]{2,1,0:T(8,128)(2,1)S(1)}, u32[]{:S(2)}, u32[]{:S(2)}) collective-permute-start(bf16[2,128,128]{2,1,0:T(8,128)(2,1)S(1)} %get-tuple-element.22), channel_id=1, source_target_pairs={{0,10},{1,11},{2,12},{3,13},{4,14},{5,15},{6,16},{7,17},{8,18},{9,... | collective-permute-start | bytes 196616 | tf_op jit(solution)/shard_map/ppermute | solution.py:189
  17.8 4.3 %collective-permute-done = bf16[2,128,128]{2,1,0:T(8,128)(2,1)S(1)} collective-permute-done((bf16[2,128,128]{2,1,0:T(8,128)(2,1)S(1)}, bf16[2,128,128]{2,1,0:T(8,128)(2,1)S(1)}, u32[]{:S(2)}, u32[]{:S(2)}) %collective-permute-start) | collective-permute-done | bytes 65568 | tf_op jit(solution)/shard_map/ppermute | solution.py:189
  22.1 10.2 %collective-permute-done.1 = bf16[2,128,128]{2,1,0:T(8,128)(2,1)S(1)} collective-permute-done((bf16[2,128,128]{2,1,0:T(8,128)(2,1)S(1)}, bf16[2,128,128]{2,1,0:T(8,128)(2,1)S(1)}, u32[]{:S(2)}, u32[]{:S(2)}) %collective-permute-start.1) | collective-permute-done | bytes 65568 | tf_op jit(solution)/shard_map/ppermute | solution.py:189
  32.3 1.9 %collective-permute-start.2 = (bf16[3,2,128,128]{3,2,1,0:T(8,128)(2,1)S(1)}, bf16[3,2,128,128]{3,2,1,0:T(8,128)(2,1)S(1)}, u32[]{:S(2)}, u32[]{:S(2)}) collective-permute-start(bf16[3,2,128,128]{3,2,1,0:T(8,128)(2,1)S(1)} %pad_maximum_fusion.2.far), channel_id=1, source_target_pairs={{0,1},{1,0},{2,3},{3,2},{4,5},{5,4},{6,7},{7,6},{8,9},{9,8},{10,11... | collective-permute-start | bytes 589832 | tf_op jit(solution)/shard_map/ppermute | solution.py:193
  34.2 1.4 %collective-permute-done.2.far_s = bf16[3,2,128,128]{3,2,1,0:T(8,128)(2,1)S(1)} collective-permute-done((bf16[3,2,128,128]{3,2,1,0:T(8,128)(2,1)S(1)}, bf16[3,2,128,128]{3,2,1,0:T(8,128)(2,1)S(1)}, u32[]{:S(2)}, u32[]{:S(2)}) %collective-permute-start.2) | collective-permute-done | bytes 196640 | tf_op jit(solution)/shard_map/ppermute | solution.py:193
  35.7 1.9 %collective-permute-start.4 = (bf16[6,2,128,128]{3,2,1,0:T(8,128)(2,1)S(1)}, bf16[6,2,128,128]{3,2,1,0:T(8,128)(2,1)S(1)}, u32[]{:S(2)}, u32[]{:S(2)}) collective-permute-start(bf16[6,2,128,128]{3,2,1,0:T(8,128)(2,1)S(1)} %pad_maximum_fusion.1), channel_id=1, source_target_pairs={{0,4},{1,29},{2,6},{3,31},{4,8},{5,1},{6,10},{7,3},{8,12},{9,5},{1... | collective-permute-start | bytes 1179656 | tf_op jit(solution)/shard_map/ppermute | solution.py:201
  37.6 1.9 %collective-permute-start.3 = (bf16[6,2,128,128]{3,2,1,0:T(8,128)(2,1)S(1)}, bf16[6,2,128,128]{3,2,1,0:T(8,128)(2,1)S(1)}, u32[]{:S(2)}, u32[]{:S(2)}) collective-permute-start(bf16[6,2,128,128]{3,2,1,0:T(8,128)(2,1)S(1)} %pad_maximum_fusion.1), channel_id=1, source_target_pairs={{0,2},{1,31},{2,4},{3,1},{4,6},{5,3},{6,8},{7,5},{8,10},{9,7},{10,... | collective-permute-start | bytes 1179656 | tf_op jit(solution)/shard_map/ppermute | solution.py:201
  39.5 7.5 %collective-permute-start.5 = (bf16[2,128,128]{2,1,0:T(8,128)(2,1)S(1)}, bf16[2,128,128]{2,1,0:T(8,128)(2,1)S(1)}, u32[]{:S(2)}, u32[]{:S(2)}) collective-permute-start(bf16[2,128,128]{2,1,0:T(8,128)(2,1)S(1)} %collective-permute-done), channel_id=1, source_target_pairs={{0,26},{1,27},{2,28},{3,29},{4,30},{5,31},{6,0},{7,1},{8,2},{9,3},... | collective-permute-start | bytes 196616 | tf_op jit(solution)/shard_map/ppermute | solution.py:189
  47.0 4.7 %collective-permute-done.5 = bf16[2,128,128]{2,1,0:T(8,128)(2,1)S(1)} collective-permute-done((bf16[2,128,128]{2,1,0:T(8,128)(2,1)S(1)}, bf16[2,128,128]{2,1,0:T(8,128)(2,1)S(1)}, u32[]{:S(2)}, u32[]{:S(2)}) %collective-permute-start.5) | collective-permute-done | bytes 65568 | tf_op jit(solution)/shard_map/ppermute | solution.py:189
  51.8 0.5 collective-permute-done.3
  52.4 5.9 %collective-permute-start.6 = (bf16[13,2,128,128]{3,2,1,0:T(8,128)(2,1)S(1)}, bf16[13,2,128,128]{3,2,1,0:T(8,128)(2,1)S(1)}, u32[]{:S(2)}, u32[]{:S(2)}) collective-permute-start(bf16[13,2,128,128]{3,2,1,0:T(8,128)(2,1)S(1)} %pad_maximum_fusion.near), channel_id=1, source_target_pairs={{0,1},{1,0},{2,3},{3,2},{4,5},{5,4},{6,7},{7,6},{8,9},{9,8},{10,11... | collective-permute-start | bytes 2555912 | tf_op jit(solution)/shard_map/ppermute | solution.py:193
  58.4 1.9 %collective-permute-done.6.near_s = bf16[13,2,128,128]{3,2,1,0:T(8,128)(2,1)S(1)} collective-permute-done((bf16[13,2,128,128]{3,2,1,0:T(8,128)(2,1)S(1)}, bf16[13,2,128,128]{3,2,1,0:T(8,128)(2,1)S(1)}, u32[]{:S(2)}, u32[]{:S(2)}) %collective-permute-start.6) | collective-permute-done | bytes 852000 | tf_op jit(solution)/shard_map/ppermute | solution.py:193
  60.3 6.0 %forward_backward.1 = (bf16[16,128,128]{2,1,0:T(8,128)(2,1)S(1)}, bf16[16,128,128]{2,1,0:T(8,128)(2,1)S(1)}, bf16[4,128,128]{2,1,0:T(8,128)(2,1)S(1)}, bf16[4,12...) custom-call(s32[1,24]{1,0:T(1,128)S(1)} %copy-done, ...), custom_call_target="tpu_custom_call" | custom-call | tf_op jit(solution)/shard_map/forward_backward/pallas_call | solution.py:161
  66.3 2.3 %collective-permute-start.7 = (bf16[16,128,128]{2,1,0:T(8,128)(2,1)S(1)}, bf16[16,128,128]{2,1,0:T(8,128)(2,1)S(1)}, u32[]{:S(2)}, u32[]{:S(2)}) collective-permute-start(bf16[16,128,128]{2,1,0:T(8,128)(2,1)S(1)} %get-tuple-element.11), channel_id=1, source_target_pairs={{0,1},{1,0},{2,3},{3,2},{4,5},{5,4},{6,7},{7,6},{8,9},{9,8},{10,11... | collective-permute-start | bytes 1572872 | tf_op jit(solution)/shard_map/ppermute | solution.py:193
  68.6 2.9 %weight_terms.1 = bf16[16,72,8,128]{3,2,1,0:T(8,128)(2,1)} custom-call(s32[1,24]{1,0:T(1,128)S(1)} %copy-done, s32[1,24]{1,0:T(1,128)S(1)} %copy-done.1, s32[1,24]{1,0:T(1,128)S(1)} %copy-done.2, s32[66]{0:T(128)S(1)} %pad_add_fusion.here, bf16[32,2,128,128]{3,2,1,0:T(8,128)(2,1)S(1)} %get-tuple-element.12.acts, ...), custom_call_target="tpu_custom_call" | custom-call | tf_op jit(solution)/shard_map/weight_terms/pallas_call | solution.py:178
  71.4 7.5 %all-to-all-start = ((bf16[16,72,8,128]{3,2,1,0:T(8,128)(2,1)}), bf16[16,72,8,128]{3,2,1,0:T(8,128)(2,1)}, u32[]{:S(2)}, u32[]{:S(2)}) async-start(bf16[16,72,8,128]{3,2,1,0:T(8,128)(2,1)} %weight_terms.1), calls=%async_computation | async-start | bytes 4718592 | tf_op jit(solution)/shard_map/all_to_all | solution.py:236
  79.1 2.5 %collective-permute-start.8 = (bf16[6,128,128]{2,1,0:T(8,128)(2,1)S(1)}, bf16[6,128,128]{2,1,0:T(8,128)(2,1)S(1)}, u32[]{:S(2)}, u32[]{:S(2)}) collective-permute-start(bf16[6,128,128]{2,1,0:T(8,128)(2,1)S(1)} %get-tuple-element.16), channel_id=1, source_target_pairs={{0,2},{1,31},{2,4},{3,1},{4,6},{5,3},{6,8},{7,5},{8,10},{9,7},{10,... | collective-permute-start | bytes 589832 | tf_op jit(solution)/shard_map/ppermute | solution.py:201
  81.6 2.4 %collective-permute-start.9 = (bf16[6,128,128]{2,1,0:T(8,128)(2,1)S(1)}, bf16[6,128,128]{2,1,0:T(8,128)(2,1)S(1)}, u32[]{:S(2)}, u32[]{:S(2)}) collective-permute-start(bf16[6,128,128]{2,1,0:T(8,128)(2,1)S(1)} %get-tuple-element.17), channel_id=1, source_target_pairs={{0,4},{1,29},{2,6},{3,31},{4,8},{5,1},{6,10},{7,3},{8,12},{9,5},{1... | collective-permute-start | bytes 589832 | tf_op jit(solution)/shard_map/ppermute | solution.py:201
  83.9 3.9 %collective-permute-done.8 = bf16[6,128,128]{2,1,0:T(8,128)(2,1)S(1)} collective-permute-done((bf16[6,128,128]{2,1,0:T(8,128)(2,1)S(1)}, bf16[6,128,128]{2,1,0:T(8,128)(2,1)S(1)}, u32[]{:S(2)}, u32[]{:S(2)}) %collective-permute-start.8) | collective-permute-done | bytes 196640 | tf_op jit(solution)/shard_map/ppermute | solution.py:201
  87.9 4.3 %collective-permute-done.9 = bf16[6,128,128]{2,1,0:T(8,128)(2,1)S(1)} collective-permute-done((bf16[6,128,128]{2,1,0:T(8,128)(2,1)S(1)}, bf16[6,128,128]{2,1,0:T(8,128)(2,1)S(1)}, u32[]{:S(2)}, u32[]{:S(2)}) %collective-permute-start.9) | collective-permute-done | bytes 196640 | tf_op jit(solution)/shard_map/ppermute | solution.py:201
  92.2 1.9 %collective-permute-start.10 = (bf16[3,128,128]{2,1,0:T(8,128)(2,1)S(1)}, bf16[3,128,128]{2,1,0:T(8,128)(2,1)S(1)}, u32[]{:S(2)}, u32[]{:S(2)}) collective-permute-start(bf16[3,128,128]{2,1,0:T(8,128)(2,1)S(1)} %add_convert_fusion.1), channel_id=1, source_target_pairs={{0,1},{1,0},{2,3},{3,2},{4,5},{5,4},{6,7},{7,6},{8,9},{9,8},{10,11... | collective-permute-start | bytes 294920 | tf_op jit(solution)/shard_map/ppermute | solution.py:193
  94.1 3.4 %collective-permute-start.11 = (bf16[128,128]{1,0:T(8,128)(2,1)S(1)}, bf16[128,128]{1,0:T(8,128)(2,1)S(1)}, u32[]{:S(2)}, u32[]{:S(2)}) collective-permute-start(bf16[128,128]{1,0:T(8,128)(2,1)S(1)} %slice_bitcast_fusion.4), channel_id=1, source_target_pairs={{0,6},{1,7},{2,8},{3,9},{4,10},{5,11},{6,12},{7,13},{8,14},{9,15},... | collective-permute-start | bytes 98312 | tf_op jit(solution)/shard_map/ppermute | solution.py:189
  97.5 6.7 %collective-permute-start.13 = (bf16[128,128]{1,0:T(8,128)(2,1)S(1)}, bf16[128,128]{1,0:T(8,128)(2,1)S(1)}, u32[]{:S(2)}, u32[]{:S(2)}) collective-permute-start(bf16[128,128]{1,0:T(8,128)(2,1)S(1)} %fusion.5), channel_id=1, source_target_pairs={{0,22},{1,23},{2,24},{3,25},{4,26},{5,27},{6,28},{7,29},{8,30},{9,... | collective-permute-start | bytes 98312 | tf_op jit(solution)/shard_map/ppermute | solution.py:189
  104.2 1.2 collective-permute-done.11
  105.4 2.8 %collective-permute-start.12 = (bf16[128,128]{1,0:T(8,128)(2,1)S(1)}, bf16[128,128]{1,0:T(8,128)(2,1)S(1)}, u32[]{:S(2)}, u32[]{:S(2)}) collective-permute-start(bf16[128,128]{1,0:T(8,128)(2,1)S(1)} %fusion), channel_id=1, source_target_pairs={{0,10},{1,11},{2,12},{3,13},{4,14},{5,15},{6,16},{7,17},{8,18},{9,... | collective-permute-start | bytes 98312 | tf_op jit(solution)/shard_map/ppermute | solution.py:189
  108.3 1.8 %collective-permute-done.13 = bf16[128,128]{1,0:T(8,128)(2,1)S(1)} collective-permute-done((bf16[128,128]{1,0:T(8,128)(2,1)S(1)}, bf16[128,128]{1,0:T(8,128)(2,1)S(1)}, u32[]{:S(2)}, u32[]{:S(2)}) %collective-permute-start.13) | collective-permute-done | bytes 32800 | tf_op jit(solution)/shard_map/ppermute | solution.py:189
  110.1 7.4 %collective-permute-done.12 = bf16[128,128]{1,0:T(8,128)(2,1)S(1)} collective-permute-done((bf16[128,128]{1,0:T(8,128)(2,1)S(1)}, bf16[128,128]{1,0:T(8,128)(2,1)S(1)}, u32[]{:S(2)}, u32[]{:S(2)}) %collective-permute-start.12) | collective-permute-done | bytes 32800 | tf_op jit(solution)/shard_map/ppermute | solution.py:189
  117.5 0.6 fusion.2
  118.1 2.0 %reduce_sum.12 = bf16[72,8,128]{2,1,0:T(8,128)(2,1)S(1)} reduce(bf16[16,72,8,128]{3,2,1,0:T(8,128)(2,1)} %all-to-all-done, bf16[]{:T(256)} %constant.35.clone.1), dimensions={0}, to_apply=%region_0.1 | reduce | flops 1105920 | bytes 2506754 | tf_op jit(solution)/shard_map/reduce_sum | solution.py:238
  120.1 0.7 slice_bitcast_fusion
  (23 shorter events, 0.5 us)
Async XLA Ops:
  0.6 57.7 %copy-start.3 = (s32[2,64]{1,0:T(2,128)S(1)}, s32[2,64]{1,0:T(2,128)}, u32[]{:S(2)}) copy-start(s32[2,64]{1,0:T(2,128)} %constant.36.clone) | copy-start | bytes 1540
  0.6 59.6 %copy-start.2 = (s32[1,24]{1,0:T(1,128)S(1)}, s32[1,24]{1,0:T(1,128)}, u32[]{:S(2)}) copy-start(s32[1,24]{1,0:T(1,128)} %dl.3) | copy-start | bytes 292
  0.7 59.6 %copy-start.1 = (s32[1,24]{1,0:T(1,128)S(1)}, s32[1,24]{1,0:T(1,128)}, u32[]{:S(2)}) copy-start(s32[1,24]{1,0:T(1,128)} %ul.3) | copy-start | bytes 292
  0.7 59.6 %copy-start = (s32[1,24]{1,0:T(1,128)S(1)}, s32[1,24]{1,0:T(1,128)}, u32[]{:S(2)}) copy-start(s32[1,24]{1,0:T(1,128)} %gl.3) | copy-start | bytes 292
  1.5 20.6 %collective-permute-start = (bf16[2,128,128]{2,1,0:T(8,128)(2,1)S(1)}, bf16[2,128,128]{2,1,0:T(8,128)(2,1)S(1)}, u32[]{:S(2)}, u32[]{:S(2)}) collective-permute-start(bf16[2,128,128]{2,1,0:T(8,128)(2,1)S(1)} %get-tuple-element.22), channel_id=1, source_target_pairs={{0,22},{1,23},{2,24},{3,25},{4,26},{5,27},{6,28},{7,29},{8,30},{9,... | collective-permute-start | bytes 196616 | tf_op jit(solution)/shard_map/ppermute | solution.py:189
  15.9 16.4 %collective-permute-start.1 = (bf16[2,128,128]{2,1,0:T(8,128)(2,1)S(1)}, bf16[2,128,128]{2,1,0:T(8,128)(2,1)S(1)}, u32[]{:S(2)}, u32[]{:S(2)}) collective-permute-start(bf16[2,128,128]{2,1,0:T(8,128)(2,1)S(1)} %get-tuple-element.22), channel_id=1, source_target_pairs={{0,10},{1,11},{2,12},{3,13},{4,14},{5,15},{6,16},{7,17},{8,18},{9,... | collective-permute-start | bytes 196616 | tf_op jit(solution)/shard_map/ppermute | solution.py:189
  32.3 3.3 %collective-permute-start.2 = (bf16[3,2,128,128]{3,2,1,0:T(8,128)(2,1)S(1)}, bf16[3,2,128,128]{3,2,1,0:T(8,128)(2,1)S(1)}, u32[]{:S(2)}, u32[]{:S(2)}) collective-permute-start(bf16[3,2,128,128]{3,2,1,0:T(8,128)(2,1)S(1)} %pad_maximum_fusion.2.far), channel_id=1, source_target_pairs={{0,1},{1,0},{2,3},{3,2},{4,5},{5,4},{6,7},{7,6},{8,9},{9,8},{10,11... | collective-permute-start | bytes 589832 | tf_op jit(solution)/shard_map/ppermute | solution.py:193
  35.7 16.1 %collective-permute-start.4 = (bf16[6,2,128,128]{3,2,1,0:T(8,128)(2,1)S(1)}, bf16[6,2,128,128]{3,2,1,0:T(8,128)(2,1)S(1)}, u32[]{:S(2)}, u32[]{:S(2)}) collective-permute-start(bf16[6,2,128,128]{3,2,1,0:T(8,128)(2,1)S(1)} %pad_maximum_fusion.1), channel_id=1, source_target_pairs={{0,4},{1,29},{2,6},{3,31},{4,8},{5,1},{6,10},{7,3},{8,12},{9,5},{1... | collective-permute-start | bytes 1179656 | tf_op jit(solution)/shard_map/ppermute | solution.py:201
  37.6 14.7 %collective-permute-start.3 = (bf16[6,2,128,128]{3,2,1,0:T(8,128)(2,1)S(1)}, bf16[6,2,128,128]{3,2,1,0:T(8,128)(2,1)S(1)}, u32[]{:S(2)}, u32[]{:S(2)}) collective-permute-start(bf16[6,2,128,128]{3,2,1,0:T(8,128)(2,1)S(1)} %pad_maximum_fusion.1), channel_id=1, source_target_pairs={{0,2},{1,31},{2,4},{3,1},{4,6},{5,3},{6,8},{7,5},{8,10},{9,7},{10,... | collective-permute-start | bytes 1179656 | tf_op jit(solution)/shard_map/ppermute | solution.py:201
  39.5 12.2 %collective-permute-start.5 = (bf16[2,128,128]{2,1,0:T(8,128)(2,1)S(1)}, bf16[2,128,128]{2,1,0:T(8,128)(2,1)S(1)}, u32[]{:S(2)}, u32[]{:S(2)}) collective-permute-start(bf16[2,128,128]{2,1,0:T(8,128)(2,1)S(1)} %collective-permute-done), channel_id=1, source_target_pairs={{0,26},{1,27},{2,28},{3,29},{4,30},{5,31},{6,0},{7,1},{8,2},{9,3},... | collective-permute-start | bytes 196616 | tf_op jit(solution)/shard_map/ppermute | solution.py:189
  52.4 7.9 %collective-permute-start.6 = (bf16[13,2,128,128]{3,2,1,0:T(8,128)(2,1)S(1)}, bf16[13,2,128,128]{3,2,1,0:T(8,128)(2,1)S(1)}, u32[]{:S(2)}, u32[]{:S(2)}) collective-permute-start(bf16[13,2,128,128]{3,2,1,0:T(8,128)(2,1)S(1)} %pad_maximum_fusion.near), channel_id=1, source_target_pairs={{0,1},{1,0},{2,3},{3,2},{4,5},{5,4},{6,7},{7,6},{8,9},{9,8},{10,11... | collective-permute-start | bytes 2555912 | tf_op jit(solution)/shard_map/ppermute | solution.py:193
  66.3 12.6 %collective-permute-start.7 = (bf16[16,128,128]{2,1,0:T(8,128)(2,1)S(1)}, bf16[16,128,128]{2,1,0:T(8,128)(2,1)S(1)}, u32[]{:S(2)}, u32[]{:S(2)}) collective-permute-start(bf16[16,128,128]{2,1,0:T(8,128)(2,1)S(1)} %get-tuple-element.11), channel_id=1, source_target_pairs={{0,1},{1,0},{2,3},{3,2},{4,5},{5,4},{6,7},{7,6},{8,9},{9,8},{10,11... | collective-permute-start | bytes 1572872 | tf_op jit(solution)/shard_map/ppermute | solution.py:193
  71.4 46.7 %all-to-all-start = ((bf16[16,72,8,128]{3,2,1,0:T(8,128)(2,1)}), bf16[16,72,8,128]{3,2,1,0:T(8,128)(2,1)}, u32[]{:S(2)}, u32[]{:S(2)}) async-start(bf16[16,72,8,128]{3,2,1,0:T(8,128)(2,1)} %weight_terms.1), calls=%async_computation | async-start | bytes 4718592 | tf_op jit(solution)/shard_map/all_to_all | solution.py:236
  79.1 8.8 %collective-permute-start.8 = (bf16[6,128,128]{2,1,0:T(8,128)(2,1)S(1)}, bf16[6,128,128]{2,1,0:T(8,128)(2,1)S(1)}, u32[]{:S(2)}, u32[]{:S(2)}) collective-permute-start(bf16[6,128,128]{2,1,0:T(8,128)(2,1)S(1)} %get-tuple-element.16), channel_id=1, source_target_pairs={{0,2},{1,31},{2,4},{3,1},{4,6},{5,3},{6,8},{7,5},{8,10},{9,7},{10,... | collective-permute-start | bytes 589832 | tf_op jit(solution)/shard_map/ppermute | solution.py:201
  81.6 10.5 %collective-permute-start.9 = (bf16[6,128,128]{2,1,0:T(8,128)(2,1)S(1)}, bf16[6,128,128]{2,1,0:T(8,128)(2,1)S(1)}, u32[]{:S(2)}, u32[]{:S(2)}) collective-permute-start(bf16[6,128,128]{2,1,0:T(8,128)(2,1)S(1)} %get-tuple-element.17), channel_id=1, source_target_pairs={{0,4},{1,29},{2,6},{3,31},{4,8},{5,1},{6,10},{7,3},{8,12},{9,5},{1... | collective-permute-start | bytes 589832 | tf_op jit(solution)/shard_map/ppermute | solution.py:201
  92.2 5.3 %collective-permute-start.10 = (bf16[3,128,128]{2,1,0:T(8,128)(2,1)S(1)}, bf16[3,128,128]{2,1,0:T(8,128)(2,1)S(1)}, u32[]{:S(2)}, u32[]{:S(2)}) collective-permute-start(bf16[3,128,128]{2,1,0:T(8,128)(2,1)S(1)} %add_convert_fusion.1), channel_id=1, source_target_pairs={{0,1},{1,0},{2,3},{3,2},{4,5},{5,4},{6,7},{7,6},{8,9},{9,8},{10,11... | collective-permute-start | bytes 294920 | tf_op jit(solution)/shard_map/ppermute | solution.py:193
  94.1 11.3 %collective-permute-start.11 = (bf16[128,128]{1,0:T(8,128)(2,1)S(1)}, bf16[128,128]{1,0:T(8,128)(2,1)S(1)}, u32[]{:S(2)}, u32[]{:S(2)}) collective-permute-start(bf16[128,128]{1,0:T(8,128)(2,1)S(1)} %slice_bitcast_fusion.4), channel_id=1, source_target_pairs={{0,6},{1,7},{2,8},{3,9},{4,10},{5,11},{6,12},{7,13},{8,14},{9,15},... | collective-permute-start | bytes 98312 | tf_op jit(solution)/shard_map/ppermute | solution.py:189
  97.5 12.5 %collective-permute-start.13 = (bf16[128,128]{1,0:T(8,128)(2,1)S(1)}, bf16[128,128]{1,0:T(8,128)(2,1)S(1)}, u32[]{:S(2)}, u32[]{:S(2)}) collective-permute-start(bf16[128,128]{1,0:T(8,128)(2,1)S(1)} %fusion.5), channel_id=1, source_target_pairs={{0,22},{1,23},{2,24},{3,25},{4,26},{5,27},{6,28},{7,29},{8,30},{9,... | collective-permute-start | bytes 98312 | tf_op jit(solution)/shard_map/ppermute | solution.py:189
  105.4 12.0 %collective-permute-start.12 = (bf16[128,128]{1,0:T(8,128)(2,1)S(1)}, bf16[128,128]{1,0:T(8,128)(2,1)S(1)}, u32[]{:S(2)}, u32[]{:S(2)}) collective-permute-start(bf16[128,128]{1,0:T(8,128)(2,1)S(1)} %fusion), channel_id=1, source_target_pairs={{0,10},{1,11},{2,12},{3,13},{4,14},{5,15},{6,16},{7,17},{8,18},{9,... | collective-permute-start | bytes 98312 | tf_op jit(solution)/shard_map/ppermute | solution.py:189

commit v3 on v2

--- a/solution.py
+++ b/solution.py
@@ -18,10 +18,9 @@
 NT = 32
 NP = 16
 UNROLL = 24
+SUM_SLOTS = 12
 NZ = 16
-FAR = (0, 5, -5)
-NEAR = (1, 2)
-OPPOSITE = 8
+NZ = 16
 
 
 def dot(a, b, ca, cb):
@@ -46,22 +45,25 @@
 
 
 def orders(core):
-    held, sent = {}, {}
-    for other in range(2):
-        for f, far in enumerate(FAR):
-            held[other * NZ + far % NZ] = other * 3 + f
-            sent[other * NZ + far % NZ] = other * 16 + 12 + f
-            for n, near in enumerate(NEAR):
-                for way in (1, -1):
-                    at = other * NZ + (way * near + far) % NZ
-                    mine = (way == 1) == (core == 0)
-                    held[at] = 19 + n * 6 + (1 - other) * 3 + f if mine else 6 + n * 6 + other * 3 + f
-                    sent[at] = n * 6 + other * 3 + f if mine else 16 + n * 6 + (1 - other) * 3 + f
-        held[other * NZ + OPPOSITE] = 31 if other else 18
-        sent[other * NZ + OPPOSITE] = 31 if other else 15
-    for table in (held, sent):
-        assert sorted(table) == sorted(table.values()) == list(range(2 * NZ))
-    return [held[i] for i in range(2 * NZ)] + [sent[i] for i in range(2 * NZ)]
+    way = 1 - 2 * core
+    behind, ahead = [0, -4 * way, 8, 4 * way], [0, 4 * way, 8, -4 * way]
+    held = [(0, o) for o in behind] + [(1, o) for o in ahead]
+    held += [(0, o - way) for o in behind] + [(1, o - way) for o in ahead]
+    held += [(0, -2 * way), (0, -6 * way), (1, -2 * way), (1, -6 * way)]
+    held += [(1, o + way) for o in ahead] + [(0, o + way) for o in behind]
+    held += [(1, 2 * way), (1, 6 * way), (0, 2 * way), (0, 6 * way)]
+    sent = [(0, o + way) for o in ahead] + [(1, o + way) for o in ahead]
+    sent += [(0, 2 * way), (0, 6 * way), (1, 2 * way), (1, 6 * way)]
+    sent += [(0, o) for o in ahead]
+    sent += [(1, o - way) for o in behind] + [(0, o - way) for o in behind]
+    sent += [(1, -2 * way), (1, -6 * way), (0, -2 * way), (0, -6 * way)]
+    sent += [(1, o) for o in behind]
+    tables = []
+    for blocks in (held, sent):
+        at = {other * NZ + offset % NZ: i for i, (other, offset) in enumerate(blocks)}
+        assert sorted(at) == list(range(2 * NZ))
+        tables += [at[i] for i in range(2 * NZ)]
+    return tables
 
 
 def place(e, here, table):
@@ -70,13 +72,15 @@
     return here[2 + table * 2 * NZ + ((d & 1) ^ here[1]) * NZ + offset]
 
 
-def forward_kernel(gl, ul, dl, here, far, far_s, near, near_s, gw, uw, dw, p_own, p_other, gg_ref, gu_ref, hid_ref, acts, acc, accp, weights, sems):
+def forward_kernel(gl, ul, dl, here, far, far_s, one, two, one_s, two_s, gw, uw, dw, p_own, p_other, gg_ref, gu_ref, hid_ref, acts, acc, accp, weights, sems):
     loads = []
     for src, start, size in (
-        (far, 0, 3),
-        (far_s, 3, 3),
-        (near, 6, 13),
-        (near_s, 19, 13),
+        (far, 0, 4),
+        (far_s, 4, 4),
+        (one, 8, 8),
+        (two, 16, 4),
+        (one_s, 20, 8),
+        (two_s, 28, 4),
     ):
         loads.append(pltpu.make_async_copy(src, acts.at[pl.ds(start, size)], sems.at[len(loads)]))
     for src, dst in (
@@ -89,11 +93,11 @@
         load.start()
     acc[...] = jnp.zeros_like(acc)
     accp[...] = jnp.zeros_like(accp)
-    for load in loads[:4]:
+    for load in loads[:6]:
         load.wait()
 
     def project(which, entries, side, contract):
-        loads[4 + which].wait()
+        loads[6 + which].wait()
 
         def add(k):
             e = entries[0, k]
@@ -149,6 +153,22 @@
     slots(down)
 
 
+def sum_kernel(got, gate, up, down, held, sems):
+    loads = []
+    for i in range(3 * NS // SUM_SLOTS):
+        part = pl.ds(i * SUM_SLOTS, SUM_SLOTS)
+        loads.append(pltpu.make_async_copy(got.at[:, part], held.at[:, part], sems.at[i]))
+        loads[-1].start()
+    for i, load in enumerate(loads):
+        load.wait()
+        part = pl.ds(i * SUM_SLOTS, SUM_SLOTS)
+        acc = held[0, part].astype(F32)
+        for p in range(1, NP):
+            acc += held[p, part].astype(F32)
+        out = (gate, up, down)[i * SUM_SLOTS // NS]
+        out[pl.ds(i * SUM_SLOTS % NS, SUM_SLOTS)] = acc.astype(BF)
+
+
 SMEM = pl.BlockSpec(memory_space=pltpu.SMEM)
 VMEM = pl.BlockSpec(memory_space=pltpu.VMEM)
 ANY = pl.BlockSpec(memory_space=pl.ANY)
@@ -160,16 +180,16 @@
     half = jax.ShapeDtypeStruct((16, NB, NB), BF)
     return pl.pallas_call(
         forward_kernel,
-        in_specs=[SMEM] * 4 + [ANY] * 4 + [HBM] * 3,
+        in_specs=[SMEM] * 4 + [ANY] * 6 + [HBM] * 3,
         out_specs=[VMEM] * 6,
         out_shape=[half, half, block, block, block, jax.ShapeDtypeStruct((DB, 2, NB, NB), BF)],
         scratch_shapes=[
             pltpu.VMEM((3, HB + 1, NB, NB), F32),
             pltpu.VMEM((DB + 1, NB, NB), F32),
             pltpu.VMEM((3, NS, NB, NB), BF),
-            pltpu.SemaphoreType.DMA((7,)),
+            pltpu.SemaphoreType.DMA((9,)),
         ],
-        compiler_params=pltpu.CompilerParams(vmem_limit_bytes=44 << 20),
+        compiler_params=pltpu.CompilerParams(vmem_limit_bytes=16 << 20),
         name="forward_backward",
     )(*lists, here, *acts, *weights)
 
@@ -185,6 +205,22 @@
     )(*lists, here, acts, gg, gu, hid)
 
 
+def sum_groups(got):
+    rows = jax.ShapeDtypeStruct((NS, NB // NP, NB), BF)
+    return pl.pallas_call(
+        sum_kernel,
+        in_specs=[ANY],
+        out_specs=[VMEM] * 3,
+        out_shape=[rows] * 3,
+        scratch_shapes=[
+            pltpu.VMEM((NP, 3 * NS, NB // NP, NB), BF),
+            pltpu.SemaphoreType.DMA((3 * NS // SUM_SLOTS,)),
+        ],
+        compiler_params=pltpu.CompilerParams(vmem_limit_bytes=8 << 20),
+        name="sum_groups",
+    )(got)
+
+
 def shift(x, steps):
     return lax.ppermute(x, "tensor", [(i, (i + 2 * steps) % NT) for i in range(NT)])
 
@@ -204,24 +240,27 @@
 def reduce_features(p_own, p_other):
     p_other = swap(p_other)
     s = total(p_own, p_other)
-    r1 = part_ways(s[:6], NEAR[0])
-    r2 = part_ways(s[6:12], NEAR[1])
-    r3 = shift(s[15], OPPOSITE - FAR[1])
-    t = [total(s[12], r1[0], r2[0]), total(s[13], r1[1], r2[1], r3), total(s[14], r1[2], r2[2])]
-    t_other = swap(total(r1[3:], r2[3:]))
-    u = [total(t[f], t_other[f]) for f in range(3)]
-    return total(u[0], shift(u[1], FAR[1]), shift(u[2], FAR[2]))
+    r1 = part_ways(s[:8], 1)
+    r2 = part_ways(s[8:12], 2)
+    own = [total(s[12 + i], r1[i], *([r2[i]] if i < 2 else [])) for i in range(4)]
+    other = [total(r1[4 + i], *([r2[2 + i]] if i < 2 else [])) for i in range(4)]
+    got = swap(jnp.stack([own[3], other[3], other[0], other[2]]))
+    r4 = part_ways(jnp.stack([total(own[1], got[1]), total(other[1], got[0])]), 4)
+    r8 = shift(total(own[2], got[3]), 8)
+    last = swap(r4[1])
+    return total(own[0], got[2], r8, r4[0], last)
 
 
 def gather_features(x):
-    far = jnp.stack([x, shift(x, -FAR[1]), shift(x, -FAR[2])])
+    opposite = shift(x, 8)
+    back = part_ways(x, 4)
+    forth = part_ways(x, -4)
+    far = jnp.stack([x, back, opposite, forth])
     far_s = swap(far)
-    full = jnp.concatenate([far, far_s])
-    one = part_ways(full, NEAR[0])
-    two = part_ways(full, NEAR[1])
-    last = shift(far[1], FAR[1] - OPPOSITE)[None]
-    near = jnp.concatenate([one, two, last])
-    return far, far_s, near, swap(near)
+    one = part_ways(jnp.concatenate([far, far_s]), 1)
+    two = part_ways(jnp.concatenate([far[:2], far_s[:1], far_s[3:]]), 2)
+    one_s = swap(one)
+    return far, far_s, one, two, one_s, swap(two)
 
 
 def on_device(inputs, cotangent, gate_w, up_w, down_w, gate_list, up_list, down_list):
@@ -235,8 +274,7 @@
     terms = weight_terms(lists, here, acts, gg, gu, hid, scale)
     got = lax.all_to_all(terms, "dp", 0, 0, tiled=True)
     grad_x = reduce_features(p_own, p_other)
-    grads = jnp.sum(got.astype(F32), axis=0).astype(BF)
-    return grad_x, grads[None, :NS], grads[None, NS : 2 * NS], grads[None, 2 * NS :]
+    return grad_x, *(g[None] for g in sum_groups(got))
 
 
 def solution(mesh):

time: 121 us -> 116 us (0.959)
  the two profiles are of different devices: /device:TPU:2 before, /device:TPU:1 now
where the time goes in v3:
time: 116 us
  starting transfers between devices  78.8 us (68%)
  waiting for transfers between devices  22.7 us (20%)
  Pallas kernels  8.03 us (7%)
  other arithmetic  3.68 us (3%)
  local copies, waits for them, and re-layouts  1.58 us (1%)
    ppermute x7, starting transfers between devices, part_ways(): lax.ppermute(x, 'tensor', [(i, (i + (2 * steps if i % 2 == 0 else -2 * st...  30.6 us
    ppermute x6, starting transfers between devices, swap(): return lax.ppermute(x, 'tensor', [(i, i ^ 1) for i in range(NT)])  21.8 us
    ppermute x2, starting transfers between devices, shift(): lax.ppermute(x, 'tensor', [(i, (i + 2 * steps) % NT) for i in range(NT)])  19.7 us
    ppermute x7, waiting for transfers between devices, part_ways(): lax.ppermute(x, 'tensor', [(i, (i + (2 * steps if i % 2 == 0 else -2 * st...  15.3 us
    all_to_all x1, starting transfers between devices, on_device(): got = lax.all_to_all(terms, 'dp', 0, 0, tiled=True)  6.78 us
    pallas_call x1, Pallas kernels, forward(): pl.pallas_call(forward_kernel, in_specs=[SMEM] * 4 + [ANY] * 6 + [HBM] *...  5.35 us
    ppermute x2, waiting for transfers between devices, shift(): lax.ppermute(x, 'tensor', [(i, (i + 2 * steps) % NT) for i in range(NT)])  4.29 us
    ppermute x6, waiting for transfers between devices, swap(): return lax.ppermute(x, 'tensor', [(i, i ^ 1) for i in range(NT)])  3.07 us
  transfers between devices with their start and end apart: 16, of which 10 were waited for; matrix products, arithmetic and copies ran while one was open for 3% of the time, Pallas kernels for 1%

profile of v3, /device:TPU:1, one launch (start us, length us, event | category | flops | bytes accessed | tf_op | source)
XLA Modules:
  0.0 115.7 jit_solution(8527288734320178295)
XLA Ops:
  0.7 0.8 fusion.3
  1.5 16.3 %collective-permute-start.1 = (bf16[2,128,128]{2,1,0:T(8,128)(2,1)S(1)}, bf16[2,128,128]{2,1,0:T(8,128)(2,1)S(1)}, u32[]{:S(2)}, u32[]{:S(2)}) collective-permute-start(bf16[2,128,128]{2,1,0:T(8,128)(2,1)S(1)} %get-tuple-element.32), channel_id=1, source_target_pairs={{0,16},{1,17},{2,18},{3,19},{4,20},{5,21},{6,22},{7,23},{8,24},{9,... | collective-permute-start | bytes 196616 | tf_op jit(solution)/shard_map/ppermute | solution.py:225
  17.8 1.9 %collective-permute-start = (bf16[2,128,128]{2,1,0:T(8,128)(2,1)S(1)}, bf16[2,128,128]{2,1,0:T(8,128)(2,1)S(1)}, u32[]{:S(2)}, u32[]{:S(2)}) collective-permute-start(bf16[2,128,128]{2,1,0:T(8,128)(2,1)S(1)} %get-tuple-element.32), channel_id=1, source_target_pairs={{0,8},{1,25},{2,10},{3,27},{4,12},{5,29},{6,14},{7,31},{8,16},{9,1... | collective-permute-start | bytes 196616 | tf_op jit(solution)/shard_map/ppermute | solution.py:237
  19.7 7.3 %collective-permute-start.2 = (bf16[2,128,128]{2,1,0:T(8,128)(2,1)S(1)}, bf16[2,128,128]{2,1,0:T(8,128)(2,1)S(1)}, u32[]{:S(2)}, u32[]{:S(2)}) collective-permute-start(bf16[2,128,128]{2,1,0:T(8,128)(2,1)S(1)} %get-tuple-element.32), channel_id=1, source_target_pairs={{0,24},{1,9},{2,26},{3,11},{4,28},{5,13},{6,30},{7,15},{8,0},{9,17... | collective-permute-start | bytes 196616 | tf_op jit(solution)/shard_map/ppermute | solution.py:237
  27.7 1.2 %collective-permute-done = bf16[2,128,128]{2,1,0:T(8,128)(2,1)S(1)} collective-permute-done((bf16[2,128,128]{2,1,0:T(8,128)(2,1)S(1)}, bf16[2,128,128]{2,1,0:T(8,128)(2,1)S(1)}, u32[]{:S(2)}, u32[]{:S(2)}) %collective-permute-start) | collective-permute-done | bytes 65568 | tf_op jit(solution)/shard_map/ppermute | solution.py:237
  28.9 1.7 %collective-permute-done.2 = bf16[2,128,128]{2,1,0:T(8,128)(2,1)S(1)} collective-permute-done((bf16[2,128,128]{2,1,0:T(8,128)(2,1)S(1)}, bf16[2,128,128]{2,1,0:T(8,128)(2,1)S(1)}, u32[]{:S(2)}, u32[]{:S(2)}) %collective-permute-start.2) | collective-permute-done | bytes 65568 | tf_op jit(solution)/shard_map/ppermute | solution.py:237
  30.7 6.0 %collective-permute-start.3 = (bf16[4,2,128,128]{3,2,1,0:T(8,128)(2,1)S(1)}, bf16[4,2,128,128]{3,2,1,0:T(8,128)(2,1)S(1)}, u32[]{:S(2)}, u32[]{:S(2)}) collective-permute-start(bf16[4,2,128,128]{3,2,1,0:T(8,128)(2,1)S(1)} %pad_maximum_fusion.far), channel_id=1, source_target_pairs={{0,1},{1,0},{2,3},{3,2},{4,5},{5,4},{6,7},{7,6},{8,9},{9,8},{10,11... | collective-permute-start | bytes 786440 | tf_op jit(solution)/shard_map/ppermute | solution.py:229
  36.8 1.1 collective-permute-done.3.far_s
  37.9 4.4 %collective-permute-start.4 = (bf16[8,2,128,128]{3,2,1,0:T(8,128)(2,1)S(1)}, bf16[8,2,128,128]{3,2,1,0:T(8,128)(2,1)S(1)}, u32[]{:S(2)}, u32[]{:S(2)}) collective-permute-start(bf16[8,2,128,128]{3,2,1,0:T(8,128)(2,1)S(1)} %constant_dynamic-update-slice_fusion), channel_id=1, source_target_pairs={{0,2},{1,31},{2,4},{3,1},{4,6},{5,3},{6,8},{7,5},{8,10},{9,7},{10,... | collective-permute-start | bytes 1572872 | tf_op jit(solution)/shard_map/ppermute | solution.py:237
  42.3 2.6 %collective-permute-start.5 = (bf16[4,2,128,128]{3,2,1,0:T(8,128)(2,1)S(1)}, bf16[4,2,128,128]{3,2,1,0:T(8,128)(2,1)S(1)}, u32[]{:S(2)}, u32[]{:S(2)}) collective-permute-start(bf16[4,2,128,128]{3,2,1,0:T(8,128)(2,1)S(1)} %pad_maximum_fusion.2), channel_id=1, source_target_pairs={{0,4},{1,29},{2,6},{3,31},{4,8},{5,1},{6,10},{7,3},{8,12},{9,5},{1... | collective-permute-start | bytes 786440 | tf_op jit(solution)/shard_map/ppermute | solution.py:237
  44.9 6.2 %collective-permute-done.4.one = bf16[8,2,128,128]{3,2,1,0:T(8,128)(2,1)S(1)} collective-permute-done((bf16[8,2,128,128]{3,2,1,0:T(8,128)(2,1)S(1)}, bf16[8,2,128,128]{3,2,1,0:T(8,128)(2,1)S(1)}, u32[]{:S(2)}, u32[]{:S(2)}) %collective-permute-start.4) | collective-permute-done | bytes 524320 | tf_op jit(solution)/shard_map/ppermute | solution.py:237
  51.1 1.9 %collective-permute-start.6 = (bf16[8,2,128,128]{3,2,1,0:T(8,128)(2,1)S(1)}, bf16[8,2,128,128]{3,2,1,0:T(8,128)(2,1)S(1)}, u32[]{:S(2)}, u32[]{:S(2)}) collective-permute-start(bf16[8,2,128,128]{3,2,1,0:T(8,128)(2,1)S(1)} %collective-permute-done.4.one), channel_id=1, source_target_pairs={{0,1},{1,0},{2,3},{3,2},{4,5},{5,4},{6,7},{7,6},{8,9},{9,8},{10,11... | collective-permute-start | bytes 1572872 | tf_op jit(solution)/shard_map/ppermute | solution.py:229
  53.0 1.0 collective-permute-done.5.two
  54.0 2.7 %collective-permute-start.7 = (bf16[4,2,128,128]{3,2,1,0:T(8,128)(2,1)S(1)}, bf16[4,2,128,128]{3,2,1,0:T(8,128)(2,1)S(1)}, u32[]{:S(2)}, u32[]{:S(2)}) collective-permute-start(bf16[4,2,128,128]{3,2,1,0:T(8,128)(2,1)S(1)} %collective-permute-done.5.two), channel_id=1, source_target_pairs={{0,1},{1,0},{2,3},{3,2},{4,5},{5,4},{6,7},{7,6},{8,9},{9,8},{10,11... | collective-permute-start | bytes 786440 | tf_op jit(solution)/shard_map/ppermute | solution.py:229
  56.9 1.0 collective-permute-done.7.two_s
  57.9 5.4 %forward_backward.1 = (bf16[16,128,128]{2,1,0:T(8,128)(2,1)S(1)}, bf16[16,128,128]{2,1,0:T(8,128)(2,1)S(1)}, bf16[4,128,128]{2,1,0:T(8,128)(2,1)S(1)}, bf16[4,12...) custom-call(s32[1,24]{1,0:T(1,128)S(1)} %copy-done.1, ...), custom_call_target="tpu_custom_call" | custom-call | tf_op jit(solution)/shard_map/forward_backward/pallas_call | solution.py:181
  63.2 2.3 %collective-permute-start.8 = (bf16[16,128,128]{2,1,0:T(8,128)(2,1)S(1)}, bf16[16,128,128]{2,1,0:T(8,128)(2,1)}, u32[]{:S(2)}, u32[]{:S(2)}) collective-permute-start(bf16[16,128,128]{2,1,0:T(8,128)(2,1)S(1)} %get-tuple-element.14), channel_id=1, source_target_pairs={{0,1},{1,0},{2,3},{3,2},{4,5},{5,4},{6,7},{7,6},{8,9},{9,8},{10,11... | collective-permute-start | bytes 1572872 | tf_op jit(solution)/shard_map/ppermute | solution.py:229
  65.5 1.4 %weight_terms.1 = bf16[16,72,8,128]{3,2,1,0:T(8,128)(2,1)S(1)} custom-call(s32[1,24]{1,0:T(1,128)S(1)} %copy-done.1, s32[1,24]{1,0:T(1,128)S(1)} %copy-done.2, s32[1,24]{1,0:T(1,128)S(1)} %copy-done.3, s32[66]{0:T(128)S(1)} %pad_add_fusion.here, bf16[32,2,128,128]{3,2,1,0:T(8,128)(2,1)S(1)} %get-tuple-element.15.acts, ...), custom_call_target="tpu_custom_call" | custom-call | tf_op jit(solution)/shard_map/weight_terms/pallas_call | solution.py:198
  67.0 1.4 %copy-done = bf16[16,72,8,128]{3,2,1,0:T(8,128)(2,1)} copy-done((bf16[16,72,8,128]{3,2,1,0:T(8,128)(2,1)}, bf16[16,72,8,128]{3,2,1,0:T(8,128)(2,1)S(1)}, u32[]{:S(2)}) %copy-start) | copy-done | bytes 2359320
  68.4 6.8 %all-to-all-start = ((bf16[16,72,8,128]{3,2,1,0:T(8,128)(2,1)}), bf16[16,72,8,128]{3,2,1,0:T(8,128)(2,1)S(1)}, u32[]{:S(2)}, u32[]{:S(2)}) async-start(bf16[16,72,8,128]{3,2,1,0:T(8,128)(2,1)} %copy-done), calls=%async_computation | async-start | bytes 4718592 | tf_op jit(solution)/shard_map/all_to_all | solution.py:275
  75.2 1.2 %add_convert_fusion = bf16[16,128,128]{2,1,0:T(8,128)(2,1)S(1)} fusion(bf16[16,128,128]{2,1,0:T(8,128)(2,1)} %collective-permute-done.8, bf16[16,128,128]{2,1,0:T(8,128)(2,1)S(1)} %get-tuple-element.13), kind=kLoop, calls=%fused_computation | loop fusion | flops 1048576 | bytes 1572864 | tf_op jit(solution)/shard_map/convert_element_type | solution.py:233
  76.4 4.5 %collective-permute-start.9 = (bf16[8,128,128]{2,1,0:T(8,128)(2,1)S(1)}, bf16[8,128,128]{2,1,0:T(8,128)(2,1)S(1)}, u32[]{:S(2)}, u32[]{:S(2)}) collective-permute-start(bf16[8,128,128]{2,1,0:T(8,128)(2,1)S(1)} %slice.109), channel_id=1, source_target_pairs={{0,2},{1,31},{2,4},{3,1},{4,6},{5,3},{6,8},{7,5},{8,10},{9,7},{10,... | collective-permute-start | bytes 786440 | tf_op jit(solution)/shard_map/ppermute | solution.py:237
  80.9 4.2 %collective-permute-start.10 = (bf16[4,128,128]{2,1,0:T(8,128)(2,1)S(1)}, bf16[4,128,128]{2,1,0:T(8,128)(2,1)S(1)}, u32[]{:S(2)}, u32[]{:S(2)}) collective-permute-start(bf16[4,128,128]{2,1,0:T(8,128)(2,1)S(1)} %slice.111), channel_id=1, source_target_pairs={{0,4},{1,29},{2,6},{3,31},{4,8},{5,1},{6,10},{7,3},{8,12},{9,5},{1... | collective-permute-start | bytes 393224 | tf_op jit(solution)/shard_map/ppermute | solution.py:237
  85.2 3.8 %collective-permute-done.10 = bf16[4,128,128]{2,1,0:T(8,128)(2,1)S(1)} collective-permute-done((bf16[4,128,128]{2,1,0:T(8,128)(2,1)S(1)}, bf16[4,128,128]{2,1,0:T(8,128)(2,1)S(1)}, u32[]{:S(2)}, u32[]{:S(2)}) %collective-permute-start.10) | collective-permute-done | bytes 131104 | tf_op jit(solution)/shard_map/ppermute | solution.py:237
  89.0 3.9 %collective-permute-start.11 = (bf16[4,128,128]{2,1,0:T(8,128)(2,1)S(1)}, bf16[4,128,128]{2,1,0:T(8,128)(2,1)S(1)}, u32[]{:S(2)}, u32[]{:S(2)}) collective-permute-start(bf16[4,128,128]{2,1,0:T(8,128)(2,1)S(1)} %pad_maximum_fusion.3), channel_id=1, source_target_pairs={{0,1},{1,0},{2,3},{3,2},{4,5},{5,4},{6,7},{7,6},{8,9},{9,8},{10,11... | collective-permute-start | bytes 393224 | tf_op jit(solution)/shard_map/ppermute | solution.py:229
  92.9 1.0 collective-permute-done.11
  94.0 5.7 %collective-permute-start.13 = (bf16[2,128,128]{2,1,0:T(8,128)(2,1)S(1)}, bf16[2,128,128]{2,1,0:T(8,128)(2,1)S(1)}, u32[]{:S(2)}, u32[]{:S(2)}) collective-permute-start(bf16[2,128,128]{2,1,0:T(8,128)(2,1)S(1)} %pad_maximum_fusion.5), channel_id=1, source_target_pairs={{0,8},{1,25},{2,10},{3,27},{4,12},{5,29},{6,14},{7,31},{8,16},{9,1... | collective-permute-start | bytes 196616 | tf_op jit(solution)/shard_map/ppermute | solution.py:237
  99.7 3.4 %collective-permute-start.12 = (bf16[128,128]{1,0:T(8,128)(2,1)S(1)}, bf16[128,128]{1,0:T(8,128)(2,1)S(1)}, u32[]{:S(2)}, u32[]{:S(2)}) collective-permute-start(bf16[128,128]{1,0:T(8,128)(2,1)S(1)} %get-tuple-element.22), channel_id=1, source_target_pairs={{0,16},{1,17},{2,18},{3,19},{4,20},{5,21},{6,22},{7,23},{8,24},{9,... | collective-permute-start | bytes 98312 | tf_op jit(solution)/shard_map/ppermute | solution.py:225
  103.1 1.5 %collective-permute-done.13 = bf16[2,128,128]{2,1,0:T(8,128)(2,1)S(1)} collective-permute-done((bf16[2,128,128]{2,1,0:T(8,128)(2,1)S(1)}, bf16[2,128,128]{2,1,0:T(8,128)(2,1)S(1)}, u32[]{:S(2)}, u32[]{:S(2)}) %collective-permute-start.13) | collective-permute-done | bytes 65568 | tf_op jit(solution)/shard_map/ppermute | solution.py:237
  104.6 4.9 %collective-permute-start.14 = (bf16[128,128]{1,0:T(8,128)(2,1)S(1)}, bf16[128,128]{1,0:T(8,128)(2,1)S(1)}, u32[]{:S(2)}, u32[]{:S(2)}) collective-permute-start(bf16[128,128]{1,0:T(8,128)(2,1)S(1)} %slice_bitcast_fusion), channel_id=1, source_target_pairs={{0,1},{1,0},{2,3},{3,2},{4,5},{5,4},{6,7},{7,6},{8,9},{9,8},{10,11... | collective-permute-start | bytes 98312 | tf_op jit(solution)/shard_map/ppermute | solution.py:229
  109.5 4.3 %collective-permute-done.12 = bf16[128,128]{1,0:T(8,128)(2,1)S(1)} collective-permute-done((bf16[128,128]{1,0:T(8,128)(2,1)S(1)}, bf16[128,128]{1,0:T(8,128)(2,1)S(1)}, u32[]{:S(2)}, u32[]{:S(2)}) %collective-permute-start.12) | collective-permute-done | bytes 32800 | tf_op jit(solution)/shard_map/ppermute | solution.py:225
  114.5 1.2 %sum_groups.1 = (bf16[24,8,128]{2,1,0:T(8,128)(2,1)}, bf16[24,8,128]{2,1,0:T(8,128)(2,1)}, bf16[24,8,128]{2,1,0:T(8,128)(2,1)}) custom-call(bf16[16,72,8,128]{3,2,1,0:T(8,128)(2,1)S(1)} %all-to-all-done.got), custom_call_target="tpu_custom_call" | custom-call | tf_op jit(solution)/shard_map/sum_groups/pallas_call | solution.py:210
  (34 shorter events, 1.9 us)
Async XLA Ops:
  0.6 56.1 %copy-start.4 = (s32[2,64]{1,0:T(2,128)S(1)}, s32[2,64]{1,0:T(2,128)}, u32[]{:S(2)}) copy-start(s32[2,64]{1,0:T(2,128)} %constant.33.clone) | copy-start | bytes 1540
  0.6 57.2 %copy-start.3 = (s32[1,24]{1,0:T(1,128)S(1)}, s32[1,24]{1,0:T(1,128)}, u32[]{:S(2)}) copy-start(s32[1,24]{1,0:T(1,128)} %dl.3) | copy-start | bytes 292
  0.7 57.2 %copy-start.2 = (s32[1,24]{1,0:T(1,128)S(1)}, s32[1,24]{1,0:T(1,128)}, u32[]{:S(2)}) copy-start(s32[1,24]{1,0:T(1,128)} %ul.3) | copy-start | bytes 292
  0.7 57.2 %copy-start.1 = (s32[1,24]{1,0:T(1,128)S(1)}, s32[1,24]{1,0:T(1,128)}, u32[]{:S(2)}) copy-start(s32[1,24]{1,0:T(1,128)} %gl.3) | copy-start | bytes 292
  1.5 26.3 %collective-permute-start.1 = (bf16[2,128,128]{2,1,0:T(8,128)(2,1)S(1)}, bf16[2,128,128]{2,1,0:T(8,128)(2,1)S(1)}, u32[]{:S(2)}, u32[]{:S(2)}) collective-permute-start(bf16[2,128,128]{2,1,0:T(8,128)(2,1)S(1)} %get-tuple-element.32), channel_id=1, source_target_pairs={{0,16},{1,17},{2,18},{3,19},{4,20},{5,21},{6,22},{7,23},{8,24},{9,... | collective-permute-start | bytes 196616 | tf_op jit(solution)/shard_map/ppermute | solution.py:225
  17.8 11.2 %collective-permute-start = (bf16[2,128,128]{2,1,0:T(8,128)(2,1)S(1)}, bf16[2,128,128]{2,1,0:T(8,128)(2,1)S(1)}, u32[]{:S(2)}, u32[]{:S(2)}) collective-permute-start(bf16[2,128,128]{2,1,0:T(8,128)(2,1)S(1)} %get-tuple-element.32), channel_id=1, source_target_pairs={{0,8},{1,25},{2,10},{3,27},{4,12},{5,29},{6,14},{7,31},{8,16},{9,1... | collective-permute-start | bytes 196616 | tf_op jit(solution)/shard_map/ppermute | solution.py:237
  19.7 11.0 %collective-permute-start.2 = (bf16[2,128,128]{2,1,0:T(8,128)(2,1)S(1)}, bf16[2,128,128]{2,1,0:T(8,128)(2,1)S(1)}, u32[]{:S(2)}, u32[]{:S(2)}) collective-permute-start(bf16[2,128,128]{2,1,0:T(8,128)(2,1)S(1)} %get-tuple-element.32), channel_id=1, source_target_pairs={{0,24},{1,9},{2,26},{3,11},{4,28},{5,13},{6,30},{7,15},{8,0},{9,17... | collective-permute-start | bytes 196616 | tf_op jit(solution)/shard_map/ppermute | solution.py:237
  30.7 7.2 %collective-permute-start.3 = (bf16[4,2,128,128]{3,2,1,0:T(8,128)(2,1)S(1)}, bf16[4,2,128,128]{3,2,1,0:T(8,128)(2,1)S(1)}, u32[]{:S(2)}, u32[]{:S(2)}) collective-permute-start(bf16[4,2,128,128]{3,2,1,0:T(8,128)(2,1)S(1)} %pad_maximum_fusion.far), channel_id=1, source_target_pairs={{0,1},{1,0},{2,3},{3,2},{4,5},{5,4},{6,7},{7,6},{8,9},{9,8},{10,11... | collective-permute-start | bytes 786440 | tf_op jit(solution)/shard_map/ppermute | solution.py:229
  37.9 13.2 %collective-permute-start.4 = (bf16[8,2,128,128]{3,2,1,0:T(8,128)(2,1)S(1)}, bf16[8,2,128,128]{3,2,1,0:T(8,128)(2,1)S(1)}, u32[]{:S(2)}, u32[]{:S(2)}) collective-permute-start(bf16[8,2,128,128]{3,2,1,0:T(8,128)(2,1)S(1)} %constant_dynamic-update-slice_fusion), channel_id=1, source_target_pairs={{0,2},{1,31},{2,4},{3,1},{4,6},{5,3},{6,8},{7,5},{8,10},{9,7},{10,... | collective-permute-start | bytes 1572872 | tf_op jit(solution)/shard_map/ppermute | solution.py:237
  42.3 11.7 %collective-permute-start.5 = (bf16[4,2,128,128]{3,2,1,0:T(8,128)(2,1)S(1)}, bf16[4,2,128,128]{3,2,1,0:T(8,128)(2,1)S(1)}, u32[]{:S(2)}, u32[]{:S(2)}) collective-permute-start(bf16[4,2,128,128]{3,2,1,0:T(8,128)(2,1)S(1)} %pad_maximum_fusion.2), channel_id=1, source_target_pairs={{0,4},{1,29},{2,6},{3,31},{4,8},{5,1},{6,10},{7,3},{8,12},{9,5},{1... | collective-permute-start | bytes 786440 | tf_op jit(solution)/shard_map/ppermute | solution.py:237
  51.1 6.8 %collective-permute-start.6 = (bf16[8,2,128,128]{3,2,1,0:T(8,128)(2,1)S(1)}, bf16[8,2,128,128]{3,2,1,0:T(8,128)(2,1)S(1)}, u32[]{:S(2)}, u32[]{:S(2)}) collective-permute-start(bf16[8,2,128,128]{3,2,1,0:T(8,128)(2,1)S(1)} %collective-permute-done.4.one), channel_id=1, source_target_pairs={{0,1},{1,0},{2,3},{3,2},{4,5},{5,4},{6,7},{7,6},{8,9},{9,8},{10,11... | collective-permute-start | bytes 1572872 | tf_op jit(solution)/shard_map/ppermute | solution.py:229
  54.0 3.9 %collective-permute-start.7 = (bf16[4,2,128,128]{3,2,1,0:T(8,128)(2,1)S(1)}, bf16[4,2,128,128]{3,2,1,0:T(8,128)(2,1)S(1)}, u32[]{:S(2)}, u32[]{:S(2)}) collective-permute-start(bf16[4,2,128,128]{3,2,1,0:T(8,128)(2,1)S(1)} %collective-permute-done.5.two), channel_id=1, source_target_pairs={{0,1},{1,0},{2,3},{3,2},{4,5},{5,4},{6,7},{7,6},{8,9},{9,8},{10,11... | collective-permute-start | bytes 786440 | tf_op jit(solution)/shard_map/ppermute | solution.py:229
  63.2 12.0 %collective-permute-start.8 = (bf16[16,128,128]{2,1,0:T(8,128)(2,1)S(1)}, bf16[16,128,128]{2,1,0:T(8,128)(2,1)}, u32[]{:S(2)}, u32[]{:S(2)}) collective-permute-start(bf16[16,128,128]{2,1,0:T(8,128)(2,1)S(1)} %get-tuple-element.14), channel_id=1, source_target_pairs={{0,1},{1,0},{2,3},{3,2},{4,5},{5,4},{6,7},{7,6},{8,9},{9,8},{10,11... | collective-permute-start | bytes 1572872 | tf_op jit(solution)/shard_map/ppermute | solution.py:229
  67.0 1.4 %copy-start = (bf16[16,72,8,128]{3,2,1,0:T(8,128)(2,1)}, bf16[16,72,8,128]{3,2,1,0:T(8,128)(2,1)S(1)}, u32[]{:S(2)}) copy-start(bf16[16,72,8,128]{3,2,1,0:T(8,128)(2,1)S(1)} %weight_terms.1) | copy-start | bytes 7077892
  68.4 46.0 %all-to-all-start = ((bf16[16,72,8,128]{3,2,1,0:T(8,128)(2,1)}), bf16[16,72,8,128]{3,2,1,0:T(8,128)(2,1)S(1)}, u32[]{:S(2)}, u32[]{:S(2)}) async-start(bf16[16,72,8,128]{3,2,1,0:T(8,128)(2,1)} %copy-done), calls=%async_computation | async-start | bytes 4718592 | tf_op jit(solution)/shard_map/all_to_all | solution.py:275
  76.4 8.7 %collective-permute-start.9 = (bf16[8,128,128]{2,1,0:T(8,128)(2,1)S(1)}, bf16[8,128,128]{2,1,0:T(8,128)(2,1)S(1)}, u32[]{:S(2)}, u32[]{:S(2)}) collective-permute-start(bf16[8,128,128]{2,1,0:T(8,128)(2,1)S(1)} %slice.109), channel_id=1, source_target_pairs={{0,2},{1,31},{2,4},{3,1},{4,6},{5,3},{6,8},{7,5},{8,10},{9,7},{10,... | collective-permute-start | bytes 786440 | tf_op jit(solution)/shard_map/ppermute | solution.py:237
  80.9 8.0 %collective-permute-start.10 = (bf16[4,128,128]{2,1,0:T(8,128)(2,1)S(1)}, bf16[4,128,128]{2,1,0:T(8,128)(2,1)S(1)}, u32[]{:S(2)}, u32[]{:S(2)}) collective-permute-start(bf16[4,128,128]{2,1,0:T(8,128)(2,1)S(1)} %slice.111), channel_id=1, source_target_pairs={{0,4},{1,29},{2,6},{3,31},{4,8},{5,1},{6,10},{7,3},{8,12},{9,5},{1... | collective-permute-start | bytes 393224 | tf_op jit(solution)/shard_map/ppermute | solution.py:237
  89.0 4.8 %collective-permute-start.11 = (bf16[4,128,128]{2,1,0:T(8,128)(2,1)S(1)}, bf16[4,128,128]{2,1,0:T(8,128)(2,1)S(1)}, u32[]{:S(2)}, u32[]{:S(2)}) collective-permute-start(bf16[4,128,128]{2,1,0:T(8,128)(2,1)S(1)} %pad_maximum_fusion.3), channel_id=1, source_target_pairs={{0,1},{1,0},{2,3},{3,2},{4,5},{5,4},{6,7},{7,6},{8,9},{9,8},{10,11... | collective-permute-start | bytes 393224 | tf_op jit(solution)/shard_map/ppermute | solution.py:229
  94.0 10.6 %collective-permute-start.13 = (bf16[2,128,128]{2,1,0:T(8,128)(2,1)S(1)}, bf16[2,128,128]{2,1,0:T(8,128)(2,1)S(1)}, u32[]{:S(2)}, u32[]{:S(2)}) collective-permute-start(bf16[2,128,128]{2,1,0:T(8,128)(2,1)S(1)} %pad_maximum_fusion.5), channel_id=1, source_target_pairs={{0,8},{1,25},{2,10},{3,27},{4,12},{5,29},{6,14},{7,31},{8,16},{9,1... | collective-permute-start | bytes 196616 | tf_op jit(solution)/shard_map/ppermute | solution.py:237
  99.7 14.2 %collective-permute-start.12 = (bf16[128,128]{1,0:T(8,128)(2,1)S(1)}, bf16[128,128]{1,0:T(8,128)(2,1)S(1)}, u32[]{:S(2)}, u32[]{:S(2)}) collective-permute-start(bf16[128,128]{1,0:T(8,128)(2,1)S(1)} %get-tuple-element.22), channel_id=1, source_target_pairs={{0,16},{1,17},{2,18},{3,19},{4,20},{5,21},{6,22},{7,23},{8,24},{9,... | collective-permute-start | bytes 98312 | tf_op jit(solution)/shard_map/ppermute | solution.py:225
  104.6 9.2 %collective-permute-start.14 = (bf16[128,128]{1,0:T(8,128)(2,1)S(1)}, bf16[128,128]{1,0:T(8,128)(2,1)S(1)}, u32[]{:S(2)}, u32[]{:S(2)}) collective-permute-start(bf16[128,128]{1,0:T(8,128)(2,1)S(1)} %slice_bitcast_fusion), channel_id=1, source_target_pairs={{0,1},{1,0},{2,3},{3,2},{4,5},{5,4},{6,7},{7,6},{8,9},{9,8},{10,11... | collective-permute-start | bytes 98312 | tf_op jit(solution)/shard_map/ppermute | solution.py:229

commit v4 on v3

--- a/solution.py
+++ b/solution.py
@@ -131,10 +131,10 @@
         p_other[i] = accp[16 + i].astype(BF)
 
 
-def terms_kernel(gl, ul, dl, here, acts, gg, gu, hid, out, *, scale):
+def terms_kernel(gl, ul, dl, here, acts, gg, gu, hid, out, held, sems, *, scale):
     def write(slot, e, product):
         live = jnp.where(e >= 0, scale, 0.0)
-        out[:, slot] = (product * live).astype(BF).reshape(NP, NB // NP, NB)
+        held[:, slot] = (product * live).astype(BF).reshape(NP, NB // NP, NB)
 
     def gate(k):
         e = gl[0, k]
@@ -148,9 +148,14 @@
         e = dl[0, k]
         write(2 * NS + k, e, dot(hid[row(e)], acts[place(e, here, 0), 1], 0, 0))
 
-    slots(gate)
-    slots(up)
-    slots(down)
+    stores = []
+    for i, project in enumerate((gate, up, down)):
+        slots(project)
+        part = pl.ds(i * NS, NS)
+        stores.append(pltpu.make_async_copy(held.at[:, part], out.at[:, part], sems.at[i]))
+        stores[-1].start()
+    for store in stores:
+        store.wait()
 
 
 def sum_kernel(got, gate, up, down, held, sems):
@@ -198,8 +203,12 @@
     return pl.pallas_call(
         functools.partial(terms_kernel, scale=scale),
         in_specs=[SMEM] * 4 + [VMEM] * 4,
-        out_specs=VMEM,
-        out_shape=jax.ShapeDtypeStruct((NP, 3 * NS, NB // NP, NB), BF),
+        out_specs=HBM,
+        out_shape=pltpu.HBM((NP, 3 * NS, NB // NP, NB), BF),
+        scratch_shapes=[
+            pltpu.VMEM((NP, 3 * NS, NB // NP, NB), BF),
+            pltpu.SemaphoreType.DMA((3,)),
+        ],
         compiler_params=pltpu.CompilerParams(vmem_limit_bytes=6 << 20),
         name="weight_terms",
     )(*lists, here, acts, gg, gu, hid)

time: 116 us -> 116 us (level)
  local copies, waits for them, and re-layouts: 1.58 us -> 0.16 us
    unnamed x13 -> x11, local copies, waits for them, and re-layouts: 1.49 us -> 0.06 us
  transfers between devices with their start and end apart: 16 -> 16, of which waited for: 10 -> 10; matrix products, arithmetic and copies ran while one was open for 3% -> 3% of each run, Pallas kernels for 1% -> 2%
where the time goes in v4:
time: 116 us; the launch traced here: 115 us
  starting transfers between devices  78.8 us (68%)
  waiting for transfers between devices  22.7 us (20%)
  Pallas kernels  9.12 us (8%)
  other arithmetic  3.73 us (3%)
    ppermute x7, starting transfers between devices, part_ways(): lax.ppermute(x, 'tensor', [(i, (i + (2 * steps if i % 2 == 0 else -2 * st...  30.6 us
    ppermute x6, starting transfers between devices, swap(): return lax.ppermute(x, 'tensor', [(i, i ^ 1) for i in range(NT)])  21.7 us
    ppermute x2, starting transfers between devices, shift(): lax.ppermute(x, 'tensor', [(i, (i + 2 * steps) % NT) for i in range(NT)])  19.7 us
    ppermute x7, waiting for transfers between devices, part_ways(): lax.ppermute(x, 'tensor', [(i, (i + (2 * steps if i % 2 == 0 else -2 * st...  15.3 us
    all_to_all x1, starting transfers between devices, on_device(): got = lax.all_to_all(terms, 'dp', 0, 0, tiled=True)  6.76 us
    pallas_call x1, Pallas kernels, forward(): pl.pallas_call(forward_kernel, in_specs=[SMEM] * 4 + [ANY] * 6 + [HBM] *...  5.4 us
    ppermute x2, waiting for transfers between devices, shift(): lax.ppermute(x, 'tensor', [(i, (i + 2 * steps) % NT) for i in range(NT)])  4.29 us
    ppermute x6, waiting for transfers between devices, swap(): return lax.ppermute(x, 'tensor', [(i, i ^ 1) for i in range(NT)])  3.07 us
  transfers between devices with their start and end apart: 16, of which 10 were waited for; matrix products, arithmetic and copies ran while one was open for 3% of the time, Pallas kernels for 2%

profile of v4, /device:TPU:1, one launch (start us, length us, event | category | flops | bytes accessed | tf_op | source)
XLA Modules:
  0.0 115.4 jit_solution(16001598625036007091)
XLA Ops:
  0.7 0.8 fusion.3
  1.5 16.3 %collective-permute-start.1 = (bf16[2,128,128]{2,1,0:T(8,128)(2,1)S(1)}, bf16[2,128,128]{2,1,0:T(8,128)(2,1)S(1)}, u32[]{:S(2)}, u32[]{:S(2)}) collective-permute-start(bf16[2,128,128]{2,1,0:T(8,128)(2,1)S(1)} %get-tuple-element.32), channel_id=1, source_target_pairs={{0,16},{1,17},{2,18},{3,19},{4,20},{5,21},{6,22},{7,23},{8,24},{9,... | collective-permute-start | bytes 196616 | tf_op jit(solution)/shard_map/ppermute | solution.py:234
  17.8 1.9 %collective-permute-start = (bf16[2,128,128]{2,1,0:T(8,128)(2,1)S(1)}, bf16[2,128,128]{2,1,0:T(8,128)(2,1)S(1)}, u32[]{:S(2)}, u32[]{:S(2)}) collective-permute-start(bf16[2,128,128]{2,1,0:T(8,128)(2,1)S(1)} %get-tuple-element.32), channel_id=1, source_target_pairs={{0,8},{1,25},{2,10},{3,27},{4,12},{5,29},{6,14},{7,31},{8,16},{9,1... | collective-permute-start | bytes 196616 | tf_op jit(solution)/shard_map/ppermute | solution.py:246
  19.7 7.3 %collective-permute-start.2 = (bf16[2,128,128]{2,1,0:T(8,128)(2,1)S(1)}, bf16[2,128,128]{2,1,0:T(8,128)(2,1)S(1)}, u32[]{:S(2)}, u32[]{:S(2)}) collective-permute-start(bf16[2,128,128]{2,1,0:T(8,128)(2,1)S(1)} %get-tuple-element.32), channel_id=1, source_target_pairs={{0,24},{1,9},{2,26},{3,11},{4,28},{5,13},{6,30},{7,15},{8,0},{9,17... | collective-permute-start | bytes 196616 | tf_op jit(solution)/shard_map/ppermute | solution.py:246
  27.0 0.8 constant_dynamic-update-slice_fusion.4
  27.7 1.2 %collective-permute-done = bf16[2,128,128]{2,1,0:T(8,128)(2,1)S(1)} collective-permute-done((bf16[2,128,128]{2,1,0:T(8,128)(2,1)S(1)}, bf16[2,128,128]{2,1,0:T(8,128)(2,1)S(1)}, u32[]{:S(2)}, u32[]{:S(2)}) %collective-permute-start) | collective-permute-done | bytes 65568 | tf_op jit(solution)/shard_map/ppermute | solution.py:246
  28.9 1.7 %collective-permute-done.2 = bf16[2,128,128]{2,1,0:T(8,128)(2,1)S(1)} collective-permute-done((bf16[2,128,128]{2,1,0:T(8,128)(2,1)S(1)}, bf16[2,128,128]{2,1,0:T(8,128)(2,1)S(1)}, u32[]{:S(2)}, u32[]{:S(2)}) %collective-permute-start.2) | collective-permute-done | bytes 65568 | tf_op jit(solution)/shard_map/ppermute | solution.py:246
  30.7 6.0 %collective-permute-start.3 = (bf16[4,2,128,128]{3,2,1,0:T(8,128)(2,1)S(1)}, bf16[4,2,128,128]{3,2,1,0:T(8,128)(2,1)S(1)}, u32[]{:S(2)}, u32[]{:S(2)}) collective-permute-start(bf16[4,2,128,128]{3,2,1,0:T(8,128)(2,1)S(1)} %pad_maximum_fusion.far), channel_id=1, source_target_pairs={{0,1},{1,0},{2,3},{3,2},{4,5},{5,4},{6,7},{7,6},{8,9},{9,8},{10,11... | collective-permute-start | bytes 786440 | tf_op jit(solution)/shard_map/ppermute | solution.py:238
  36.8 1.1 collective-permute-done.3.far_s
  37.9 4.4 %collective-permute-start.4 = (bf16[8,2,128,128]{3,2,1,0:T(8,128)(2,1)S(1)}, bf16[8,2,128,128]{3,2,1,0:T(8,128)(2,1)S(1)}, u32[]{:S(2)}, u32[]{:S(2)}) collective-permute-start(bf16[8,2,128,128]{3,2,1,0:T(8,128)(2,1)S(1)} %constant_dynamic-update-slice_fusion), channel_id=1, source_target_pairs={{0,2},{1,31},{2,4},{3,1},{4,6},{5,3},{6,8},{7,5},{8,10},{9,7},{10,... | collective-permute-start | bytes 1572872 | tf_op jit(solution)/shard_map/ppermute | solution.py:246
  42.3 2.6 %collective-permute-start.5 = (bf16[4,2,128,128]{3,2,1,0:T(8,128)(2,1)S(1)}, bf16[4,2,128,128]{3,2,1,0:T(8,128)(2,1)S(1)}, u32[]{:S(2)}, u32[]{:S(2)}) collective-permute-start(bf16[4,2,128,128]{3,2,1,0:T(8,128)(2,1)S(1)} %pad_maximum_fusion.2), channel_id=1, source_target_pairs={{0,4},{1,29},{2,6},{3,31},{4,8},{5,1},{6,10},{7,3},{8,12},{9,5},{1... | collective-permute-start | bytes 786440 | tf_op jit(solution)/shard_map/ppermute | solution.py:246
  44.9 6.2 %collective-permute-done.4.one = bf16[8,2,128,128]{3,2,1,0:T(8,128)(2,1)S(1)} collective-permute-done((bf16[8,2,128,128]{3,2,1,0:T(8,128)(2,1)S(1)}, bf16[8,2,128,128]{3,2,1,0:T(8,128)(2,1)S(1)}, u32[]{:S(2)}, u32[]{:S(2)}) %collective-permute-start.4) | collective-permute-done | bytes 524320 | tf_op jit(solution)/shard_map/ppermute | solution.py:246
  51.1 1.9 %collective-permute-start.6 = (bf16[8,2,128,128]{3,2,1,0:T(8,128)(2,1)S(1)}, bf16[8,2,128,128]{3,2,1,0:T(8,128)(2,1)S(1)}, u32[]{:S(2)}, u32[]{:S(2)}) collective-permute-start(bf16[8,2,128,128]{3,2,1,0:T(8,128)(2,1)S(1)} %collective-permute-done.4.one), channel_id=1, source_target_pairs={{0,1},{1,0},{2,3},{3,2},{4,5},{5,4},{6,7},{7,6},{8,9},{9,8},{10,11... | collective-permute-start | bytes 1572872 | tf_op jit(solution)/shard_map/ppermute | solution.py:238
  53.0 1.0 collective-permute-done.5.two
  54.0 2.7 %collective-permute-start.7 = (bf16[4,2,128,128]{3,2,1,0:T(8,128)(2,1)S(1)}, bf16[4,2,128,128]{3,2,1,0:T(8,128)(2,1)S(1)}, u32[]{:S(2)}, u32[]{:S(2)}) collective-permute-start(bf16[4,2,128,128]{3,2,1,0:T(8,128)(2,1)S(1)} %collective-permute-done.5.two), channel_id=1, source_target_pairs={{0,1},{1,0},{2,3},{3,2},{4,5},{5,4},{6,7},{7,6},{8,9},{9,8},{10,11... | collective-permute-start | bytes 786440 | tf_op jit(solution)/shard_map/ppermute | solution.py:238
  56.9 1.0 collective-permute-done.7.two_s
  57.9 5.4 %forward_backward.1 = (bf16[16,128,128]{2,1,0:T(8,128)(2,1)S(1)}, bf16[16,128,128]{2,1,0:T(8,128)(2,1)S(1)}, bf16[4,128,128]{2,1,0:T(8,128)(2,1)S(1)}, bf16[4,12...) custom-call(s32[1,24]{1,0:T(1,128)S(1)} %copy-done, ...), custom_call_target="tpu_custom_call" | custom-call | tf_op jit(solution)/shard_map/forward_backward/pallas_call | solution.py:186
  63.3 2.3 %collective-permute-start.8 = (bf16[16,128,128]{2,1,0:T(8,128)(2,1)S(1)}, bf16[16,128,128]{2,1,0:T(8,128)(2,1)}, u32[]{:S(2)}, u32[]{:S(2)}) collective-permute-start(bf16[16,128,128]{2,1,0:T(8,128)(2,1)S(1)} %get-tuple-element.14), channel_id=1, source_target_pairs={{0,1},{1,0},{2,3},{3,2},{4,5},{5,4},{6,7},{7,6},{8,9},{9,8},{10,11... | collective-permute-start | bytes 1572872 | tf_op jit(solution)/shard_map/ppermute | solution.py:238
  65.6 2.5 %weight_terms.1 = bf16[16,72,8,128]{3,2,1,0:T(8,128)(2,1)} custom-call(s32[1,24]{1,0:T(1,128)S(1)} %copy-done, s32[1,24]{1,0:T(1,128)S(1)} %copy-done.1, s32[1,24]{1,0:T(1,128)S(1)} %copy-done.2, s32[66]{0:T(128)S(1)} %pad_add_fusion.here, bf16[32,2,128,128]{3,2,1,0:T(8,128)(2,1)S(1)} %get-tuple-element.15.acts, ...), custom_call_target="tpu_custom_call" | custom-call | tf_op jit(solution)/shard_map/weight_terms/pallas_call | solution.py:203
  68.1 6.8 %all-to-all-start = ((bf16[16,72,8,128]{3,2,1,0:T(8,128)(2,1)}), bf16[16,72,8,128]{3,2,1,0:T(8,128)(2,1)S(1)}, u32[]{:S(2)}, u32[]{:S(2)}) async-start(bf16[16,72,8,128]{3,2,1,0:T(8,128)(2,1)} %weight_terms.1), calls=%async_computation | async-start | bytes 4718592 | tf_op jit(solution)/shard_map/all_to_all | solution.py:284
  74.9 1.2 %add_convert_fusion = bf16[16,128,128]{2,1,0:T(8,128)(2,1)S(1)} fusion(bf16[16,128,128]{2,1,0:T(8,128)(2,1)} %collective-permute-done.8, bf16[16,128,128]{2,1,0:T(8,128)(2,1)S(1)} %get-tuple-element.13), kind=kLoop, calls=%fused_computation | loop fusion | flops 1048576 | bytes 1572864 | tf_op jit(solution)/shard_map/convert_element_type | solution.py:242
  76.1 4.5 %collective-permute-start.9 = (bf16[8,128,128]{2,1,0:T(8,128)(2,1)S(1)}, bf16[8,128,128]{2,1,0:T(8,128)(2,1)S(1)}, u32[]{:S(2)}, u32[]{:S(2)}) collective-permute-start(bf16[8,128,128]{2,1,0:T(8,128)(2,1)S(1)} %slice.109), channel_id=1, source_target_pairs={{0,2},{1,31},{2,4},{3,1},{4,6},{5,3},{6,8},{7,5},{8,10},{9,7},{10,... | collective-permute-start | bytes 786440 | tf_op jit(solution)/shard_map/ppermute | solution.py:246
  80.6 4.2 %collective-permute-start.10 = (bf16[4,128,128]{2,1,0:T(8,128)(2,1)S(1)}, bf16[4,128,128]{2,1,0:T(8,128)(2,1)S(1)}, u32[]{:S(2)}, u32[]{:S(2)}) collective-permute-start(bf16[4,128,128]{2,1,0:T(8,128)(2,1)S(1)} %slice.111), channel_id=1, source_target_pairs={{0,4},{1,29},{2,6},{3,31},{4,8},{5,1},{6,10},{7,3},{8,12},{9,5},{1... | collective-permute-start | bytes 393224 | tf_op jit(solution)/shard_map/ppermute | solution.py:246
  84.9 3.8 %collective-permute-done.10 = bf16[4,128,128]{2,1,0:T(8,128)(2,1)S(1)} collective-permute-done((bf16[4,128,128]{2,1,0:T(8,128)(2,1)S(1)}, bf16[4,128,128]{2,1,0:T(8,128)(2,1)S(1)}, u32[]{:S(2)}, u32[]{:S(2)}) %collective-permute-start.10) | collective-permute-done | bytes 131104 | tf_op jit(solution)/shard_map/ppermute | solution.py:246
  88.7 3.9 %collective-permute-start.11 = (bf16[4,128,128]{2,1,0:T(8,128)(2,1)S(1)}, bf16[4,128,128]{2,1,0:T(8,128)(2,1)S(1)}, u32[]{:S(2)}, u32[]{:S(2)}) collective-permute-start(bf16[4,128,128]{2,1,0:T(8,128)(2,1)S(1)} %pad_maximum_fusion.3), channel_id=1, source_target_pairs={{0,1},{1,0},{2,3},{3,2},{4,5},{5,4},{6,7},{7,6},{8,9},{9,8},{10,11... | collective-permute-start | bytes 393224 | tf_op jit(solution)/shard_map/ppermute | solution.py:238
  92.6 1.0 collective-permute-done.11
  93.7 5.7 %collective-permute-start.13 = (bf16[2,128,128]{2,1,0:T(8,128)(2,1)S(1)}, bf16[2,128,128]{2,1,0:T(8,128)(2,1)S(1)}, u32[]{:S(2)}, u32[]{:S(2)}) collective-permute-start(bf16[2,128,128]{2,1,0:T(8,128)(2,1)S(1)} %pad_maximum_fusion.5), channel_id=1, source_target_pairs={{0,8},{1,25},{2,10},{3,27},{4,12},{5,29},{6,14},{7,31},{8,16},{9,1... | collective-permute-start | bytes 196616 | tf_op jit(solution)/shard_map/ppermute | solution.py:246
  99.3 3.4 %collective-permute-start.12 = (bf16[128,128]{1,0:T(8,128)(2,1)S(1)}, bf16[128,128]{1,0:T(8,128)(2,1)S(1)}, u32[]{:S(2)}, u32[]{:S(2)}) collective-permute-start(bf16[128,128]{1,0:T(8,128)(2,1)S(1)} %get-tuple-element.22), channel_id=1, source_target_pairs={{0,16},{1,17},{2,18},{3,19},{4,20},{5,21},{6,22},{7,23},{8,24},{9,... | collective-permute-start | bytes 98312 | tf_op jit(solution)/shard_map/ppermute | solution.py:234
  102.8 1.5 %collective-permute-done.13 = bf16[2,128,128]{2,1,0:T(8,128)(2,1)S(1)} collective-permute-done((bf16[2,128,128]{2,1,0:T(8,128)(2,1)S(1)}, bf16[2,128,128]{2,1,0:T(8,128)(2,1)S(1)}, u32[]{:S(2)}, u32[]{:S(2)}) %collective-permute-start.13) | collective-permute-done | bytes 65568 | tf_op jit(solution)/shard_map/ppermute | solution.py:246
  104.3 4.9 %collective-permute-start.14 = (bf16[128,128]{1,0:T(8,128)(2,1)S(1)}, bf16[128,128]{1,0:T(8,128)(2,1)S(1)}, u32[]{:S(2)}, u32[]{:S(2)}) collective-permute-start(bf16[128,128]{1,0:T(8,128)(2,1)S(1)} %slice_bitcast_fusion), channel_id=1, source_target_pairs={{0,1},{1,0},{2,3},{3,2},{4,5},{5,4},{6,7},{7,6},{8,9},{9,8},{10,11... | collective-permute-start | bytes 98312 | tf_op jit(solution)/shard_map/ppermute | solution.py:238
  109.2 4.3 %collective-permute-done.12 = bf16[128,128]{1,0:T(8,128)(2,1)S(1)} collective-permute-done((bf16[128,128]{1,0:T(8,128)(2,1)S(1)}, bf16[128,128]{1,0:T(8,128)(2,1)S(1)}, u32[]{:S(2)}, u32[]{:S(2)}) %collective-permute-start.12) | collective-permute-done | bytes 32800 | tf_op jit(solution)/shard_map/ppermute | solution.py:234
  114.2 1.2 %sum_groups.1 = (bf16[24,8,128]{2,1,0:T(8,128)(2,1)}, bf16[24,8,128]{2,1,0:T(8,128)(2,1)}, bf16[24,8,128]{2,1,0:T(8,128)(2,1)}) custom-call(bf16[16,72,8,128]{3,2,1,0:T(8,128)(2,1)S(1)} %all-to-all-done.got), custom_call_target="tpu_custom_call" | custom-call | tf_op jit(solution)/shard_map/sum_groups/pallas_call | solution.py:219
  (32 shorter events, 1.1 us)
Async XLA Ops:
  0.6 56.1 %copy-start.3 = (s32[2,64]{1,0:T(2,128)S(1)}, s32[2,64]{1,0:T(2,128)}, u32[]{:S(2)}) copy-start(s32[2,64]{1,0:T(2,128)} %constant.33.clone) | copy-start | bytes 1540
  0.6 57.2 %copy-start.2 = (s32[1,24]{1,0:T(1,128)S(1)}, s32[1,24]{1,0:T(1,128)}, u32[]{:S(2)}) copy-start(s32[1,24]{1,0:T(1,128)} %dl.3) | copy-start | bytes 292
  0.7 57.2 %copy-start.1 = (s32[1,24]{1,0:T(1,128)S(1)}, s32[1,24]{1,0:T(1,128)}, u32[]{:S(2)}) copy-start(s32[1,24]{1,0:T(1,128)} %ul.3) | copy-start | bytes 292
  0.7 57.2 %copy-start = (s32[1,24]{1,0:T(1,128)S(1)}, s32[1,24]{1,0:T(1,128)}, u32[]{:S(2)}) copy-start(s32[1,24]{1,0:T(1,128)} %gl.3) | copy-start | bytes 292
  1.5 26.3 %collective-permute-start.1 = (bf16[2,128,128]{2,1,0:T(8,128)(2,1)S(1)}, bf16[2,128,128]{2,1,0:T(8,128)(2,1)S(1)}, u32[]{:S(2)}, u32[]{:S(2)}) collective-permute-start(bf16[2,128,128]{2,1,0:T(8,128)(2,1)S(1)} %get-tuple-element.32), channel_id=1, source_target_pairs={{0,16},{1,17},{2,18},{3,19},{4,20},{5,21},{6,22},{7,23},{8,24},{9,... | collective-permute-start | bytes 196616 | tf_op jit(solution)/shard_map/ppermute | solution.py:234
  17.8 11.2 %collective-permute-start = (bf16[2,128,128]{2,1,0:T(8,128)(2,1)S(1)}, bf16[2,128,128]{2,1,0:T(8,128)(2,1)S(1)}, u32[]{:S(2)}, u32[]{:S(2)}) collective-permute-start(bf16[2,128,128]{2,1,0:T(8,128)(2,1)S(1)} %get-tuple-element.32), channel_id=1, source_target_pairs={{0,8},{1,25},{2,10},{3,27},{4,12},{5,29},{6,14},{7,31},{8,16},{9,1... | collective-permute-start | bytes 196616 | tf_op jit(solution)/shard_map/ppermute | solution.py:246
  19.7 11.0 %collective-permute-start.2 = (bf16[2,128,128]{2,1,0:T(8,128)(2,1)S(1)}, bf16[2,128,128]{2,1,0:T(8,128)(2,1)S(1)}, u32[]{:S(2)}, u32[]{:S(2)}) collective-permute-start(bf16[2,128,128]{2,1,0:T(8,128)(2,1)S(1)} %get-tuple-element.32), channel_id=1, source_target_pairs={{0,24},{1,9},{2,26},{3,11},{4,28},{5,13},{6,30},{7,15},{8,0},{9,17... | collective-permute-start | bytes 196616 | tf_op jit(solution)/shard_map/ppermute | solution.py:246
  30.7 7.2 %collective-permute-start.3 = (bf16[4,2,128,128]{3,2,1,0:T(8,128)(2,1)S(1)}, bf16[4,2,128,128]{3,2,1,0:T(8,128)(2,1)S(1)}, u32[]{:S(2)}, u32[]{:S(2)}) collective-permute-start(bf16[4,2,128,128]{3,2,1,0:T(8,128)(2,1)S(1)} %pad_maximum_fusion.far), channel_id=1, source_target_pairs={{0,1},{1,0},{2,3},{3,2},{4,5},{5,4},{6,7},{7,6},{8,9},{9,8},{10,11... | collective-permute-start | bytes 786440 | tf_op jit(solution)/shard_map/ppermute | solution.py:238
  37.9 13.2 %collective-permute-start.4 = (bf16[8,2,128,128]{3,2,1,0:T(8,128)(2,1)S(1)}, bf16[8,2,128,128]{3,2,1,0:T(8,128)(2,1)S(1)}, u32[]{:S(2)}, u32[]{:S(2)}) collective-permute-start(bf16[8,2,128,128]{3,2,1,0:T(8,128)(2,1)S(1)} %constant_dynamic-update-slice_fusion), channel_id=1, source_target_pairs={{0,2},{1,31},{2,4},{3,1},{4,6},{5,3},{6,8},{7,5},{8,10},{9,7},{10,... | collective-permute-start | bytes 1572872 | tf_op jit(solution)/shard_map/ppermute | solution.py:246
  42.3 11.7 %collective-permute-start.5 = (bf16[4,2,128,128]{3,2,1,0:T(8,128)(2,1)S(1)}, bf16[4,2,128,128]{3,2,1,0:T(8,128)(2,1)S(1)}, u32[]{:S(2)}, u32[]{:S(2)}) collective-permute-start(bf16[4,2,128,128]{3,2,1,0:T(8,128)(2,1)S(1)} %pad_maximum_fusion.2), channel_id=1, source_target_pairs={{0,4},{1,29},{2,6},{3,31},{4,8},{5,1},{6,10},{7,3},{8,12},{9,5},{1... | collective-permute-start | bytes 786440 | tf_op jit(solution)/shard_map/ppermute | solution.py:246
  51.1 6.8 %collective-permute-start.6 = (bf16[8,2,128,128]{3,2,1,0:T(8,128)(2,1)S(1)}, bf16[8,2,128,128]{3,2,1,0:T(8,128)(2,1)S(1)}, u32[]{:S(2)}, u32[]{:S(2)}) collective-permute-start(bf16[8,2,128,128]{3,2,1,0:T(8,128)(2,1)S(1)} %collective-permute-done.4.one), channel_id=1, source_target_pairs={{0,1},{1,0},{2,3},{3,2},{4,5},{5,4},{6,7},{7,6},{8,9},{9,8},{10,11... | collective-permute-start | bytes 1572872 | tf_op jit(solution)/shard_map/ppermute | solution.py:238
  54.0 3.9 %collective-permute-start.7 = (bf16[4,2,128,128]{3,2,1,0:T(8,128)(2,1)S(1)}, bf16[4,2,128,128]{3,2,1,0:T(8,128)(2,1)S(1)}, u32[]{:S(2)}, u32[]{:S(2)}) collective-permute-start(bf16[4,2,128,128]{3,2,1,0:T(8,128)(2,1)S(1)} %collective-permute-done.5.two), channel_id=1, source_target_pairs={{0,1},{1,0},{2,3},{3,2},{4,5},{5,4},{6,7},{7,6},{8,9},{9,8},{10,11... | collective-permute-start | bytes 786440 | tf_op jit(solution)/shard_map/ppermute | solution.py:238
  63.3 11.6 %collective-permute-start.8 = (bf16[16,128,128]{2,1,0:T(8,128)(2,1)S(1)}, bf16[16,128,128]{2,1,0:T(8,128)(2,1)}, u32[]{:S(2)}, u32[]{:S(2)}) collective-permute-start(bf16[16,128,128]{2,1,0:T(8,128)(2,1)S(1)} %get-tuple-element.14), channel_id=1, source_target_pairs={{0,1},{1,0},{2,3},{3,2},{4,5},{5,4},{6,7},{7,6},{8,9},{9,8},{10,11... | collective-permute-start | bytes 1572872 | tf_op jit(solution)/shard_map/ppermute | solution.py:238
  68.1 46.1 %all-to-all-start = ((bf16[16,72,8,128]{3,2,1,0:T(8,128)(2,1)}), bf16[16,72,8,128]{3,2,1,0:T(8,128)(2,1)S(1)}, u32[]{:S(2)}, u32[]{:S(2)}) async-start(bf16[16,72,8,128]{3,2,1,0:T(8,128)(2,1)} %weight_terms.1), calls=%async_computation | async-start | bytes 4718592 | tf_op jit(solution)/shard_map/all_to_all | solution.py:284
  76.1 8.8 %collective-permute-start.9 = (bf16[8,128,128]{2,1,0:T(8,128)(2,1)S(1)}, bf16[8,128,128]{2,1,0:T(8,128)(2,1)S(1)}, u32[]{:S(2)}, u32[]{:S(2)}) collective-permute-start(bf16[8,128,128]{2,1,0:T(8,128)(2,1)S(1)} %slice.109), channel_id=1, source_target_pairs={{0,2},{1,31},{2,4},{3,1},{4,6},{5,3},{6,8},{7,5},{8,10},{9,7},{10,... | collective-permute-start | bytes 786440 | tf_op jit(solution)/shard_map/ppermute | solution.py:246
  80.6 8.1 %collective-permute-start.10 = (bf16[4,128,128]{2,1,0:T(8,128)(2,1)S(1)}, bf16[4,128,128]{2,1,0:T(8,128)(2,1)S(1)}, u32[]{:S(2)}, u32[]{:S(2)}) collective-permute-start(bf16[4,128,128]{2,1,0:T(8,128)(2,1)S(1)} %slice.111), channel_id=1, source_target_pairs={{0,4},{1,29},{2,6},{3,31},{4,8},{5,1},{6,10},{7,3},{8,12},{9,5},{1... | collective-permute-start | bytes 393224 | tf_op jit(solution)/shard_map/ppermute | solution.py:246
  88.7 4.8 %collective-permute-start.11 = (bf16[4,128,128]{2,1,0:T(8,128)(2,1)S(1)}, bf16[4,128,128]{2,1,0:T(8,128)(2,1)S(1)}, u32[]{:S(2)}, u32[]{:S(2)}) collective-permute-start(bf16[4,128,128]{2,1,0:T(8,128)(2,1)S(1)} %pad_maximum_fusion.3), channel_id=1, source_target_pairs={{0,1},{1,0},{2,3},{3,2},{4,5},{5,4},{6,7},{7,6},{8,9},{9,8},{10,11... | collective-permute-start | bytes 393224 | tf_op jit(solution)/shard_map/ppermute | solution.py:238
  93.7 10.6 %collective-permute-start.13 = (bf16[2,128,128]{2,1,0:T(8,128)(2,1)S(1)}, bf16[2,128,128]{2,1,0:T(8,128)(2,1)S(1)}, u32[]{:S(2)}, u32[]{:S(2)}) collective-permute-start(bf16[2,128,128]{2,1,0:T(8,128)(2,1)S(1)} %pad_maximum_fusion.5), channel_id=1, source_target_pairs={{0,8},{1,25},{2,10},{3,27},{4,12},{5,29},{6,14},{7,31},{8,16},{9,1... | collective-permute-start | bytes 196616 | tf_op jit(solution)/shard_map/ppermute | solution.py:246
  99.3 14.2 %collective-permute-start.12 = (bf16[128,128]{1,0:T(8,128)(2,1)S(1)}, bf16[128,128]{1,0:T(8,128)(2,1)S(1)}, u32[]{:S(2)}, u32[]{:S(2)}) collective-permute-start(bf16[128,128]{1,0:T(8,128)(2,1)S(1)} %get-tuple-element.22), channel_id=1, source_target_pairs={{0,16},{1,17},{2,18},{3,19},{4,20},{5,21},{6,22},{7,23},{8,24},{9,... | collective-permute-start | bytes 98312 | tf_op jit(solution)/shard_map/ppermute | solution.py:234
  104.3 9.2 %collective-permute-start.14 = (bf16[128,128]{1,0:T(8,128)(2,1)S(1)}, bf16[128,128]{1,0:T(8,128)(2,1)S(1)}, u32[]{:S(2)}, u32[]{:S(2)}) collective-permute-start(bf16[128,128]{1,0:T(8,128)(2,1)S(1)} %slice_bitcast_fusion), channel_id=1, source_target_pairs={{0,1},{1,0},{2,3},{3,2},{4,5},{5,4},{6,7},{7,6},{8,9},{9,8},{10,11... | collective-permute-start | bytes 98312 | tf_op jit(solution)/shard_map/ppermute | solution.py:238

commit v5 on v4

--- a/solution.py
+++ b/solution.py
@@ -73,31 +73,23 @@
 
 
 def forward_kernel(gl, ul, dl, here, far, far_s, one, two, one_s, two_s, gw, uw, dw, p_own, p_other, gg_ref, gu_ref, hid_ref, acts, acc, accp, weights, sems):
-    loads = []
-    for src, start, size in (
-        (far, 0, 4),
-        (far_s, 4, 4),
-        (one, 8, 8),
-        (two, 16, 4),
-        (one_s, 20, 8),
-        (two_s, 28, 4),
-    ):
-        loads.append(pltpu.make_async_copy(src, acts.at[pl.ds(start, size)], sems.at[len(loads)]))
-    for src, dst in (
-        (gw.at[0], weights.at[0]),
-        (uw.at[0], weights.at[1]),
-        (dw.at[0], weights.at[2]),
-    ):
-        loads.append(pltpu.make_async_copy(src, dst, sems.at[len(loads)]))
-    for load in loads:
+    pieces = ((far, 0, 4), (far_s, 4, 4), (one, 8, 8), (two, 16, 4), (one_s, 20, 8), (two_s, 28, 4))
+
+    def bring(i, side):
+        src, start, size = pieces[i]
+        return pltpu.make_async_copy(src.at[:, side], acts.at[pl.ds(start, size), side], sems.at[6 * side + i])
+
+    sides = [[bring(i, side) for i in range(6)] for side in range(2)]
+    heavy = [pltpu.make_async_copy(w.at[0], weights.at[i], sems.at[12 + i]) for i, w in enumerate((gw, uw, dw))]
+    for load in (heavy[0], *sides[0], heavy[1], *sides[1], heavy[2]):
         load.start()
     acc[...] = jnp.zeros_like(acc)
     accp[...] = jnp.zeros_like(accp)
-    for load in loads[:6]:
+    for load in sides[0]:
         load.wait()
 
     def project(which, entries, side, contract):
-        loads[6 + which].wait()
+        heavy[which].wait()
 
         def add(k):
             e = entries[0, k]
@@ -108,6 +100,8 @@
 
     project(0, gl, 0, 0)
     project(1, ul, 0, 0)
+    for load in sides[1]:
+        load.wait()
     project(2, dl, 1, 1)
     for r in range(HB):
         gate, up, gh = acc[0, r], acc[1, r], acc[2, r]
@@ -192,7 +186,7 @@
             pltpu.VMEM((3, HB + 1, NB, NB), F32),
             pltpu.VMEM((DB + 1, NB, NB), F32),
             pltpu.VMEM((3, NS, NB, NB), BF),
-            pltpu.SemaphoreType.DMA((9,)),
+            pltpu.SemaphoreType.DMA((15,)),
         ],
         compiler_params=pltpu.CompilerParams(vmem_limit_bytes=16 << 20),
         name="forward_backward",

time: 116 us -> 116 us (level)
  waiting for transfers between devices: 22.7 us -> 21.2 us
  starting transfers between devices: 78.8 us -> 80.2 us
    ppermute x7, waiting for transfers between devices: 15.3 us -> 13.8 us  [part_ways(): lax.ppermute(x, 'tensor', [(i, (i + (2 * steps if i % 2 == 0 else -2 * st...]
    ppermute x6, starting transfers between devices: 21.7 us -> 23.2 us  [swap(): return lax.ppermute(x, 'tensor', [(i, i ^ 1) for i in range(NT)])]
  transfers between devices with their start and end apart: 16 -> 16, of which waited for: 10 -> 9; matrix products, arithmetic and copies ran while one was open for 3% -> 3% of each run, Pallas kernels for 2% -> 2%
where the time goes in v5:
time: 116 us; the launch traced here: 115 us
  starting transfers between devices  80.2 us (69%)
  waiting for transfers between devices  21.2 us (18%)
  Pallas kernels  9.05 us (8%)
  other arithmetic  3.73 us (3%)
    ppermute x7, starting transfers between devices, part_ways(): lax.ppermute(x, 'tensor', [(i, (i + (2 * steps if i % 2 == 0 else -2 * st...  30.6 us
    ppermute x6, starting transfers between devices, swap(): return lax.ppermute(x, 'tensor', [(i, i ^ 1) for i in range(NT)])  23.2 us
    ppermute x2, starting transfers between devices, shift(): lax.ppermute(x, 'tensor', [(i, (i + 2 * steps) % NT) for i in range(NT)])  19.7 us
    ppermute x7, waiting for transfers between devices, part_ways(): lax.ppermute(x, 'tensor', [(i, (i + (2 * steps if i % 2 == 0 else -2 * st...  13.8 us
    all_to_all x1, starting transfers between devices, on_device(): got = lax.all_to_all(terms, 'dp', 0, 0, tiled=True)  6.76 us
    pallas_call x1, Pallas kernels, forward(): pl.pallas_call(forward_kernel, in_specs=[SMEM] * 4 + [ANY] * 6 + [HBM] *...  5.33 us
    ppermute x2, waiting for transfers between devices, shift(): lax.ppermute(x, 'tensor', [(i, (i + 2 * steps) % NT) for i in range(NT)])  4.29 us
    ppermute x6, waiting for transfers between devices, swap(): return lax.ppermute(x, 'tensor', [(i, i ^ 1) for i in range(NT)])  3.07 us
  transfers between devices with their start and end apart: 16, of which 9 were waited for; matrix products, arithmetic and copies ran while one was open for 3% of the time, Pallas kernels for 2%

profile of v5, /device:TPU:1, one launch (start us, length us, event | category | flops | bytes accessed | tf_op | source)
XLA Modules:
  0.0 115.3 jit_solution(10898858355806372059)
XLA Ops:
  0.7 0.8 fusion.3
  1.5 16.3 %collective-permute-start.1 = (bf16[2,128,128]{2,1,0:T(8,128)(2,1)S(1)}, bf16[2,128,128]{2,1,0:T(8,128)(2,1)S(1)}, u32[]{:S(2)}, u32[]{:S(2)}) collective-permute-start(bf16[2,128,128]{2,1,0:T(8,128)(2,1)S(1)} %get-tuple-element.32), channel_id=1, source_target_pairs={{0,16},{1,17},{2,18},{3,19},{4,20},{5,21},{6,22},{7,23},{8,24},{9,... | collective-permute-start | bytes 196616 | tf_op jit(solution)/shard_map/ppermute | solution.py:228
  17.8 1.9 %collective-permute-start = (bf16[2,128,128]{2,1,0:T(8,128)(2,1)S(1)}, bf16[2,128,128]{2,1,0:T(8,128)(2,1)S(1)}, u32[]{:S(2)}, u32[]{:S(2)}) collective-permute-start(bf16[2,128,128]{2,1,0:T(8,128)(2,1)S(1)} %get-tuple-element.32), channel_id=1, source_target_pairs={{0,8},{1,25},{2,10},{3,27},{4,12},{5,29},{6,14},{7,31},{8,16},{9,1... | collective-permute-start | bytes 196616 | tf_op jit(solution)/shard_map/ppermute | solution.py:240
  19.7 7.3 %collective-permute-start.2 = (bf16[2,128,128]{2,1,0:T(8,128)(2,1)S(1)}, bf16[2,128,128]{2,1,0:T(8,128)(2,1)S(1)}, u32[]{:S(2)}, u32[]{:S(2)}) collective-permute-start(bf16[2,128,128]{2,1,0:T(8,128)(2,1)S(1)} %get-tuple-element.32), channel_id=1, source_target_pairs={{0,24},{1,9},{2,26},{3,11},{4,28},{5,13},{6,30},{7,15},{8,0},{9,17... | collective-permute-start | bytes 196616 | tf_op jit(solution)/shard_map/ppermute | solution.py:240
  27.0 0.8 constant_dynamic-update-slice_fusion.4
  27.7 1.2 %collective-permute-done = bf16[2,128,128]{2,1,0:T(8,128)(2,1)S(1)} collective-permute-done((bf16[2,128,128]{2,1,0:T(8,128)(2,1)S(1)}, bf16[2,128,128]{2,1,0:T(8,128)(2,1)S(1)}, u32[]{:S(2)}, u32[]{:S(2)}) %collective-permute-start) | collective-permute-done | bytes 65568 | tf_op jit(solution)/shard_map/ppermute | solution.py:240
  28.9 1.7 %collective-permute-done.2 = bf16[2,128,128]{2,1,0:T(8,128)(2,1)S(1)} collective-permute-done((bf16[2,128,128]{2,1,0:T(8,128)(2,1)S(1)}, bf16[2,128,128]{2,1,0:T(8,128)(2,1)S(1)}, u32[]{:S(2)}, u32[]{:S(2)}) %collective-permute-start.2) | collective-permute-done | bytes 65568 | tf_op jit(solution)/shard_map/ppermute | solution.py:240
  30.7 6.0 %collective-permute-start.3 = (bf16[4,2,128,128]{3,2,1,0:T(8,128)(2,1)S(1)}, bf16[4,2,128,128]{3,2,1,0:T(8,128)(2,1)S(1)}, u32[]{:S(2)}, u32[]{:S(2)}) collective-permute-start(bf16[4,2,128,128]{3,2,1,0:T(8,128)(2,1)S(1)} %pad_maximum_fusion.far), channel_id=1, source_target_pairs={{0,1},{1,0},{2,3},{3,2},{4,5},{5,4},{6,7},{7,6},{8,9},{9,8},{10,11... | collective-permute-start | bytes 786440 | tf_op jit(solution)/shard_map/ppermute | solution.py:232
  36.8 1.1 collective-permute-done.3.far_s
  37.9 4.4 %collective-permute-start.4 = (bf16[8,2,128,128]{3,2,1,0:T(8,128)(2,1)S(1)}, bf16[8,2,128,128]{3,2,1,0:T(8,128)(2,1)S(1)}, u32[]{:S(2)}, u32[]{:S(2)}) collective-permute-start(bf16[8,2,128,128]{3,2,1,0:T(8,128)(2,1)S(1)} %constant_dynamic-update-slice_fusion), channel_id=1, source_target_pairs={{0,2},{1,31},{2,4},{3,1},{4,6},{5,3},{6,8},{7,5},{8,10},{9,7},{10,... | collective-permute-start | bytes 1572872 | tf_op jit(solution)/shard_map/ppermute | solution.py:240
  42.3 2.6 %collective-permute-start.5 = (bf16[4,2,128,128]{3,2,1,0:T(8,128)(2,1)S(1)}, bf16[4,2,128,128]{3,2,1,0:T(8,128)(2,1)S(1)}, u32[]{:S(2)}, u32[]{:S(2)}) collective-permute-start(bf16[4,2,128,128]{3,2,1,0:T(8,128)(2,1)S(1)} %pad_maximum_fusion.2), channel_id=1, source_target_pairs={{0,4},{1,29},{2,6},{3,31},{4,8},{5,1},{6,10},{7,3},{8,12},{9,5},{1... | collective-permute-start | bytes 786440 | tf_op jit(solution)/shard_map/ppermute | solution.py:240
  44.9 6.2 %collective-permute-done.4.one = bf16[8,2,128,128]{3,2,1,0:T(8,128)(2,1)S(1)} collective-permute-done((bf16[8,2,128,128]{3,2,1,0:T(8,128)(2,1)S(1)}, bf16[8,2,128,128]{3,2,1,0:T(8,128)(2,1)S(1)}, u32[]{:S(2)}, u32[]{:S(2)}) %collective-permute-start.4) | collective-permute-done | bytes 524320 | tf_op jit(solution)/shard_map/ppermute | solution.py:240
  51.1 1.9 %collective-permute-start.6 = (bf16[8,2,128,128]{3,2,1,0:T(8,128)(2,1)S(1)}, bf16[8,2,128,128]{3,2,1,0:T(8,128)(2,1)S(1)}, u32[]{:S(2)}, u32[]{:S(2)}) collective-permute-start(bf16[8,2,128,128]{3,2,1,0:T(8,128)(2,1)S(1)} %collective-permute-done.4.one), channel_id=1, source_target_pairs={{0,1},{1,0},{2,3},{3,2},{4,5},{5,4},{6,7},{7,6},{8,9},{9,8},{10,11... | collective-permute-start | bytes 1572872 | tf_op jit(solution)/shard_map/ppermute | solution.py:232
  53.0 1.0 collective-permute-done.5.two
  54.0 2.7 %collective-permute-start.7 = (bf16[4,2,128,128]{3,2,1,0:T(8,128)(2,1)S(1)}, bf16[4,2,128,128]{3,2,1,0:T(8,128)(2,1)S(1)}, u32[]{:S(2)}, u32[]{:S(2)}) collective-permute-start(bf16[4,2,128,128]{3,2,1,0:T(8,128)(2,1)S(1)} %collective-permute-done.5.two), channel_id=1, source_target_pairs={{0,1},{1,0},{2,3},{3,2},{4,5},{5,4},{6,7},{7,6},{8,9},{9,8},{10,11... | collective-permute-start | bytes 786440 | tf_op jit(solution)/shard_map/ppermute | solution.py:232
  56.9 1.0 collective-permute-done.7.two_s
  57.9 5.3 %forward_backward.1 = (bf16[16,128,128]{2,1,0:T(8,128)(2,1)S(1)}, bf16[16,128,128]{2,1,0:T(8,128)(2,1)S(1)}, bf16[4,128,128]{2,1,0:T(8,128)(2,1)S(1)}, bf16[4,12...) custom-call(s32[1,24]{1,0:T(1,128)S(1)} %copy-done, ...), custom_call_target="tpu_custom_call" | custom-call | tf_op jit(solution)/shard_map/forward_backward/pallas_call | solution.py:180
  63.2 2.3 %collective-permute-start.8 = (bf16[16,128,128]{2,1,0:T(8,128)(2,1)S(1)}, bf16[16,128,128]{2,1,0:T(8,128)(2,1)}, u32[]{:S(2)}, u32[]{:S(2)}) collective-permute-start(bf16[16,128,128]{2,1,0:T(8,128)(2,1)S(1)} %get-tuple-element.14), channel_id=1, source_target_pairs={{0,1},{1,0},{2,3},{3,2},{4,5},{5,4},{6,7},{7,6},{8,9},{9,8},{10,11... | collective-permute-start | bytes 1572872 | tf_op jit(solution)/shard_map/ppermute | solution.py:232
  65.5 2.5 %weight_terms.1 = bf16[16,72,8,128]{3,2,1,0:T(8,128)(2,1)} custom-call(s32[1,24]{1,0:T(1,128)S(1)} %copy-done, s32[1,24]{1,0:T(1,128)S(1)} %copy-done.1, s32[1,24]{1,0:T(1,128)S(1)} %copy-done.2, s32[66]{0:T(128)S(1)} %pad_add_fusion.here, bf16[32,2,128,128]{3,2,1,0:T(8,128)(2,1)S(1)} %get-tuple-element.15.acts, ...), custom_call_target="tpu_custom_call" | custom-call | tf_op jit(solution)/shard_map/weight_terms/pallas_call | solution.py:197
  68.0 6.8 %all-to-all-start = ((bf16[16,72,8,128]{3,2,1,0:T(8,128)(2,1)}), bf16[16,72,8,128]{3,2,1,0:T(8,128)(2,1)S(1)}, u32[]{:S(2)}, u32[]{:S(2)}) async-start(bf16[16,72,8,128]{3,2,1,0:T(8,128)(2,1)} %weight_terms.1), calls=%async_computation | async-start | bytes 4718592 | tf_op jit(solution)/shard_map/all_to_all | solution.py:278
  74.8 1.2 %add_convert_fusion = bf16[16,128,128]{2,1,0:T(8,128)(2,1)S(1)} fusion(bf16[16,128,128]{2,1,0:T(8,128)(2,1)} %collective-permute-done.8, bf16[16,128,128]{2,1,0:T(8,128)(2,1)S(1)} %get-tuple-element.13), kind=kLoop, calls=%fused_computation | loop fusion | flops 1048576 | bytes 1572864 | tf_op jit(solution)/shard_map/convert_element_type | solution.py:236
  76.0 4.5 %collective-permute-start.9 = (bf16[8,128,128]{2,1,0:T(8,128)(2,1)S(1)}, bf16[8,128,128]{2,1,0:T(8,128)(2,1)S(1)}, u32[]{:S(2)}, u32[]{:S(2)}) collective-permute-start(bf16[8,128,128]{2,1,0:T(8,128)(2,1)S(1)} %slice.109), channel_id=1, source_target_pairs={{0,2},{1,31},{2,4},{3,1},{4,6},{5,3},{6,8},{7,5},{8,10},{9,7},{10,... | collective-permute-start | bytes 786440 | tf_op jit(solution)/shard_map/ppermute | solution.py:240
  80.6 4.2 %collective-permute-start.10 = (bf16[4,128,128]{2,1,0:T(8,128)(2,1)S(1)}, bf16[4,128,128]{2,1,0:T(8,128)(2,1)S(1)}, u32[]{:S(2)}, u32[]{:S(2)}) collective-permute-start(bf16[4,128,128]{2,1,0:T(8,128)(2,1)S(1)} %slice.111), channel_id=1, source_target_pairs={{0,4},{1,29},{2,6},{3,31},{4,8},{5,1},{6,10},{7,3},{8,12},{9,5},{1... | collective-permute-start | bytes 393224 | tf_op jit(solution)/shard_map/ppermute | solution.py:240
  84.8 3.8 %collective-permute-done.10 = bf16[4,128,128]{2,1,0:T(8,128)(2,1)S(1)} collective-permute-done((bf16[4,128,128]{2,1,0:T(8,128)(2,1)S(1)}, bf16[4,128,128]{2,1,0:T(8,128)(2,1)S(1)}, u32[]{:S(2)}, u32[]{:S(2)}) %collective-permute-start.10) | collective-permute-done | bytes 131104 | tf_op jit(solution)/shard_map/ppermute | solution.py:240
  88.7 3.9 %collective-permute-start.11 = (bf16[4,128,128]{2,1,0:T(8,128)(2,1)S(1)}, bf16[4,128,128]{2,1,0:T(8,128)(2,1)S(1)}, u32[]{:S(2)}, u32[]{:S(2)}) collective-permute-start(bf16[4,128,128]{2,1,0:T(8,128)(2,1)S(1)} %pad_maximum_fusion.3), channel_id=1, source_target_pairs={{0,1},{1,0},{2,3},{3,2},{4,5},{5,4},{6,7},{7,6},{8,9},{9,8},{10,11... | collective-permute-start | bytes 393224 | tf_op jit(solution)/shard_map/ppermute | solution.py:232
  92.5 1.0 collective-permute-done.11
  93.6 5.7 %collective-permute-start.13 = (bf16[2,128,128]{2,1,0:T(8,128)(2,1)S(1)}, bf16[2,128,128]{2,1,0:T(8,128)(2,1)S(1)}, u32[]{:S(2)}, u32[]{:S(2)}) collective-permute-start(bf16[2,128,128]{2,1,0:T(8,128)(2,1)S(1)} %pad_maximum_fusion.5), channel_id=1, source_target_pairs={{0,8},{1,25},{2,10},{3,27},{4,12},{5,29},{6,14},{7,31},{8,16},{9,1... | collective-permute-start | bytes 196616 | tf_op jit(solution)/shard_map/ppermute | solution.py:240
  99.3 3.4 %collective-permute-start.12 = (bf16[128,128]{1,0:T(8,128)(2,1)S(1)}, bf16[128,128]{1,0:T(8,128)(2,1)S(1)}, u32[]{:S(2)}, u32[]{:S(2)}) collective-permute-start(bf16[128,128]{1,0:T(8,128)(2,1)S(1)} %get-tuple-element.22), channel_id=1, source_target_pairs={{0,16},{1,17},{2,18},{3,19},{4,20},{5,21},{6,22},{7,23},{8,24},{9,... | collective-permute-start | bytes 98312 | tf_op jit(solution)/shard_map/ppermute | solution.py:228
  102.7 6.4 %collective-permute-start.14 = (bf16[128,128]{1,0:T(8,128)(2,1)S(1)}, bf16[128,128]{1,0:T(8,128)(2,1)S(1)}, u32[]{:S(2)}, u32[]{:S(2)}) collective-permute-start(bf16[128,128]{1,0:T(8,128)(2,1)S(1)} %slice_bitcast_fusion), channel_id=1, source_target_pairs={{0,1},{1,0},{2,3},{3,2},{4,5},{5,4},{6,7},{7,6},{8,9},{9,8},{10,11... | collective-permute-start | bytes 98312 | tf_op jit(solution)/shard_map/ppermute | solution.py:232
  109.1 4.3 %collective-permute-done.12 = bf16[128,128]{1,0:T(8,128)(2,1)S(1)} collective-permute-done((bf16[128,128]{1,0:T(8,128)(2,1)S(1)}, bf16[128,128]{1,0:T(8,128)(2,1)S(1)}, u32[]{:S(2)}, u32[]{:S(2)}) %collective-permute-start.12) | collective-permute-done | bytes 32800 | tf_op jit(solution)/shard_map/ppermute | solution.py:228
  113.4 0.7 fusion.1
  114.1 1.2 %sum_groups.1 = (bf16[24,8,128]{2,1,0:T(8,128)(2,1)}, bf16[24,8,128]{2,1,0:T(8,128)(2,1)}, bf16[24,8,128]{2,1,0:T(8,128)(2,1)}) custom-call(bf16[16,72,8,128]{3,2,1,0:T(8,128)(2,1)S(1)} %all-to-all-done.got), custom_call_target="tpu_custom_call" | custom-call | tf_op jit(solution)/shard_map/sum_groups/pallas_call | solution.py:213
  (32 shorter events, 0.4 us)
Async XLA Ops:
  0.6 56.1 %copy-start.3 = (s32[2,64]{1,0:T(2,128)S(1)}, s32[2,64]{1,0:T(2,128)}, u32[]{:S(2)}) copy-start(s32[2,64]{1,0:T(2,128)} %constant.33.clone) | copy-start | bytes 1540
  0.6 57.2 %copy-start.2 = (s32[1,24]{1,0:T(1,128)S(1)}, s32[1,24]{1,0:T(1,128)}, u32[]{:S(2)}) copy-start(s32[1,24]{1,0:T(1,128)} %dl.3) | copy-start | bytes 292
  0.7 57.2 %copy-start.1 = (s32[1,24]{1,0:T(1,128)S(1)}, s32[1,24]{1,0:T(1,128)}, u32[]{:S(2)}) copy-start(s32[1,24]{1,0:T(1,128)} %ul.3) | copy-start | bytes 292
  0.7 57.2 %copy-start = (s32[1,24]{1,0:T(1,128)S(1)}, s32[1,24]{1,0:T(1,128)}, u32[]{:S(2)}) copy-start(s32[1,24]{1,0:T(1,128)} %gl.3) | copy-start | bytes 292
  1.5 26.3 %collective-permute-start.1 = (bf16[2,128,128]{2,1,0:T(8,128)(2,1)S(1)}, bf16[2,128,128]{2,1,0:T(8,128)(2,1)S(1)}, u32[]{:S(2)}, u32[]{:S(2)}) collective-permute-start(bf16[2,128,128]{2,1,0:T(8,128)(2,1)S(1)} %get-tuple-element.32), channel_id=1, source_target_pairs={{0,16},{1,17},{2,18},{3,19},{4,20},{5,21},{6,22},{7,23},{8,24},{9,... | collective-permute-start | bytes 196616 | tf_op jit(solution)/shard_map/ppermute | solution.py:228
  17.8 11.2 %collective-permute-start = (bf16[2,128,128]{2,1,0:T(8,128)(2,1)S(1)}, bf16[2,128,128]{2,1,0:T(8,128)(2,1)S(1)}, u32[]{:S(2)}, u32[]{:S(2)}) collective-permute-start(bf16[2,128,128]{2,1,0:T(8,128)(2,1)S(1)} %get-tuple-element.32), channel_id=1, source_target_pairs={{0,8},{1,25},{2,10},{3,27},{4,12},{5,29},{6,14},{7,31},{8,16},{9,1... | collective-permute-start | bytes 196616 | tf_op jit(solution)/shard_map/ppermute | solution.py:240
  19.7 11.0 %collective-permute-start.2 = (bf16[2,128,128]{2,1,0:T(8,128)(2,1)S(1)}, bf16[2,128,128]{2,1,0:T(8,128)(2,1)S(1)}, u32[]{:S(2)}, u32[]{:S(2)}) collective-permute-start(bf16[2,128,128]{2,1,0:T(8,128)(2,1)S(1)} %get-tuple-element.32), channel_id=1, source_target_pairs={{0,24},{1,9},{2,26},{3,11},{4,28},{5,13},{6,30},{7,15},{8,0},{9,17... | collective-permute-start | bytes 196616 | tf_op jit(solution)/shard_map/ppermute | solution.py:240
  30.7 7.2 %collective-permute-start.3 = (bf16[4,2,128,128]{3,2,1,0:T(8,128)(2,1)S(1)}, bf16[4,2,128,128]{3,2,1,0:T(8,128)(2,1)S(1)}, u32[]{:S(2)}, u32[]{:S(2)}) collective-permute-start(bf16[4,2,128,128]{3,2,1,0:T(8,128)(2,1)S(1)} %pad_maximum_fusion.far), channel_id=1, source_target_pairs={{0,1},{1,0},{2,3},{3,2},{4,5},{5,4},{6,7},{7,6},{8,9},{9,8},{10,11... | collective-permute-start | bytes 786440 | tf_op jit(solution)/shard_map/ppermute | solution.py:232
  37.9 13.2 %collective-permute-start.4 = (bf16[8,2,128,128]{3,2,1,0:T(8,128)(2,1)S(1)}, bf16[8,2,128,128]{3,2,1,0:T(8,128)(2,1)S(1)}, u32[]{:S(2)}, u32[]{:S(2)}) collective-permute-start(bf16[8,2,128,128]{3,2,1,0:T(8,128)(2,1)S(1)} %constant_dynamic-update-slice_fusion), channel_id=1, source_target_pairs={{0,2},{1,31},{2,4},{3,1},{4,6},{5,3},{6,8},{7,5},{8,10},{9,7},{10,... | collective-permute-start | bytes 1572872 | tf_op jit(solution)/shard_map/ppermute | solution.py:240
  42.3 11.7 %collective-permute-start.5 = (bf16[4,2,128,128]{3,2,1,0:T(8,128)(2,1)S(1)}, bf16[4,2,128,128]{3,2,1,0:T(8,128)(2,1)S(1)}, u32[]{:S(2)}, u32[]{:S(2)}) collective-permute-start(bf16[4,2,128,128]{3,2,1,0:T(8,128)(2,1)S(1)} %pad_maximum_fusion.2), channel_id=1, source_target_pairs={{0,4},{1,29},{2,6},{3,31},{4,8},{5,1},{6,10},{7,3},{8,12},{9,5},{1... | collective-permute-start | bytes 786440 | tf_op jit(solution)/shard_map/ppermute | solution.py:240
  51.1 6.8 %collective-permute-start.6 = (bf16[8,2,128,128]{3,2,1,0:T(8,128)(2,1)S(1)}, bf16[8,2,128,128]{3,2,1,0:T(8,128)(2,1)S(1)}, u32[]{:S(2)}, u32[]{:S(2)}) collective-permute-start(bf16[8,2,128,128]{3,2,1,0:T(8,128)(2,1)S(1)} %collective-permute-done.4.one), channel_id=1, source_target_pairs={{0,1},{1,0},{2,3},{3,2},{4,5},{5,4},{6,7},{7,6},{8,9},{9,8},{10,11... | collective-permute-start | bytes 1572872 | tf_op jit(solution)/shard_map/ppermute | solution.py:232
  54.0 3.9 %collective-permute-start.7 = (bf16[4,2,128,128]{3,2,1,0:T(8,128)(2,1)S(1)}, bf16[4,2,128,128]{3,2,1,0:T(8,128)(2,1)S(1)}, u32[]{:S(2)}, u32[]{:S(2)}) collective-permute-start(bf16[4,2,128,128]{3,2,1,0:T(8,128)(2,1)S(1)} %collective-permute-done.5.two), channel_id=1, source_target_pairs={{0,1},{1,0},{2,3},{3,2},{4,5},{5,4},{6,7},{7,6},{8,9},{9,8},{10,11... | collective-permute-start | bytes 786440 | tf_op jit(solution)/shard_map/ppermute | solution.py:232
  63.2 11.6 %collective-permute-start.8 = (bf16[16,128,128]{2,1,0:T(8,128)(2,1)S(1)}, bf16[16,128,128]{2,1,0:T(8,128)(2,1)}, u32[]{:S(2)}, u32[]{:S(2)}) collective-permute-start(bf16[16,128,128]{2,1,0:T(8,128)(2,1)S(1)} %get-tuple-element.14), channel_id=1, source_target_pairs={{0,1},{1,0},{2,3},{3,2},{4,5},{5,4},{6,7},{7,6},{8,9},{9,8},{10,11... | collective-permute-start | bytes 1572872 | tf_op jit(solution)/shard_map/ppermute | solution.py:232
  68.0 46.1 %all-to-all-start = ((bf16[16,72,8,128]{3,2,1,0:T(8,128)(2,1)}), bf16[16,72,8,128]{3,2,1,0:T(8,128)(2,1)S(1)}, u32[]{:S(2)}, u32[]{:S(2)}) async-start(bf16[16,72,8,128]{3,2,1,0:T(8,128)(2,1)} %weight_terms.1), calls=%async_computation | async-start | bytes 4718592 | tf_op jit(solution)/shard_map/all_to_all | solution.py:278
  76.0 8.8 %collective-permute-start.9 = (bf16[8,128,128]{2,1,0:T(8,128)(2,1)S(1)}, bf16[8,128,128]{2,1,0:T(8,128)(2,1)S(1)}, u32[]{:S(2)}, u32[]{:S(2)}) collective-permute-start(bf16[8,128,128]{2,1,0:T(8,128)(2,1)S(1)} %slice.109), channel_id=1, source_target_pairs={{0,2},{1,31},{2,4},{3,1},{4,6},{5,3},{6,8},{7,5},{8,10},{9,7},{10,... | collective-permute-start | bytes 786440 | tf_op jit(solution)/shard_map/ppermute | solution.py:240
  80.6 8.1 %collective-permute-start.10 = (bf16[4,128,128]{2,1,0:T(8,128)(2,1)S(1)}, bf16[4,128,128]{2,1,0:T(8,128)(2,1)S(1)}, u32[]{:S(2)}, u32[]{:S(2)}) collective-permute-start(bf16[4,128,128]{2,1,0:T(8,128)(2,1)S(1)} %slice.111), channel_id=1, source_target_pairs={{0,4},{1,29},{2,6},{3,31},{4,8},{5,1},{6,10},{7,3},{8,12},{9,5},{1... | collective-permute-start | bytes 393224 | tf_op jit(solution)/shard_map/ppermute | solution.py:240
  88.7 4.8 %collective-permute-start.11 = (bf16[4,128,128]{2,1,0:T(8,128)(2,1)S(1)}, bf16[4,128,128]{2,1,0:T(8,128)(2,1)S(1)}, u32[]{:S(2)}, u32[]{:S(2)}) collective-permute-start(bf16[4,128,128]{2,1,0:T(8,128)(2,1)S(1)} %pad_maximum_fusion.3), channel_id=1, source_target_pairs={{0,1},{1,0},{2,3},{3,2},{4,5},{5,4},{6,7},{7,6},{8,9},{9,8},{10,11... | collective-permute-start | bytes 393224 | tf_op jit(solution)/shard_map/ppermute | solution.py:232
  93.6 9.1 %collective-permute-start.13 = (bf16[2,128,128]{2,1,0:T(8,128)(2,1)S(1)}, bf16[2,128,128]{2,1,0:T(8,128)(2,1)S(1)}, u32[]{:S(2)}, u32[]{:S(2)}) collective-permute-start(bf16[2,128,128]{2,1,0:T(8,128)(2,1)S(1)} %pad_maximum_fusion.5), channel_id=1, source_target_pairs={{0,8},{1,25},{2,10},{3,27},{4,12},{5,29},{6,14},{7,31},{8,16},{9,1... | collective-permute-start | bytes 196616 | tf_op jit(solution)/shard_map/ppermute | solution.py:240
  99.3 14.2 %collective-permute-start.12 = (bf16[128,128]{1,0:T(8,128)(2,1)S(1)}, bf16[128,128]{1,0:T(8,128)(2,1)S(1)}, u32[]{:S(2)}, u32[]{:S(2)}) collective-permute-start(bf16[128,128]{1,0:T(8,128)(2,1)S(1)} %get-tuple-element.22), channel_id=1, source_target_pairs={{0,16},{1,17},{2,18},{3,19},{4,20},{5,21},{6,22},{7,23},{8,24},{9,... | collective-permute-start | bytes 98312 | tf_op jit(solution)/shard_map/ppermute | solution.py:228
  102.7 10.7 %collective-permute-start.14 = (bf16[128,128]{1,0:T(8,128)(2,1)S(1)}, bf16[128,128]{1,0:T(8,128)(2,1)S(1)}, u32[]{:S(2)}, u32[]{:S(2)}) collective-permute-start(bf16[128,128]{1,0:T(8,128)(2,1)S(1)} %slice_bitcast_fusion), channel_id=1, source_target_pairs={{0,1},{1,0},{2,3},{3,2},{4,5},{5,4},{6,7},{7,6},{8,9},{9,8},{10,11... | collective-permute-start | bytes 98312 | tf_op jit(solution)/shard_map/ppermute | solution.py:232
